TPU v7x, 32 devices: a whole 2x2x4 slice. The times are simulated.
32 devices in a mesh: dev: 32 (over z, y, x, core).
Axes of the slice: x: 2, y: 2, z: 4, core: 2. Of those that a mesh axis runs over, the one named last changes fastest.
Arguments:
- factors: bfloat16 [256, 192, 256], P('dev'), may hold values from -6 to 6
- orbital_owner: int32 [256], replicated, may hold values from 0 to 31, as said below
- tile_orbitals: int32 [256, 7], P('dev'), may hold values from 0 to 255, as said below
- projectors: bfloat16 [3072, 192, 128], P('dev'), may hold values from -0.4375 to 0.4375
- amplitudes: float32 [3072, 128, 128], P('dev'), may hold values from -0.3125 to 0.3125
- ranks: int32 [3072], P('dev'), may hold values from 32 to 128, as said below
- pair_energies: float32 [3072, 128], P('dev'), may hold values from 0.5 to 4
- orbital_energies: float32 [256], replicated, may hold values from 0.25 to 2
Outputs:
- new_amplitudes: float32 [3072, 128, 128], P('dev')
- orbital_sums: bfloat16 [256, 192, 256], P('dev')
Inputs may be any that keep to these rules, and one draw needn't show every extreme that they name: `orbital_owner`: orbitals o and o + 32 have the same owner, and each device owns 8 orbitals. `tile_orbitals`: rows 8 d to 8 d + 7 are the tiles of device d. A row holds 4 consecutive orbital numbers, then 3 consecutive ones; its 12 pairs are rows 12 t + 3 a + b of the pair arrays. The tiles of one device name no orbital twice, and at most 2 orbitals of one owner; some device reaches 2 in every draw. `ranks`: some pair has rank 128.
All inputs are finite; a program needn't handle non-finite values.
Results may differ from a plain program's by a relative error of at most 0.007.
Values may be sent and summed in bfloat16 or wider, within the bound.
A program may use at most 128 MiB of HBM per device.

v0:
```python
import jax
import jax.numpy as jnp
from jax import lax
from jax.sharding import PartitionSpec as P


def pack_slots(source_table, slot_rows, slot_valid):
    picked = source_table[slot_rows]
    return jnp.where(slot_valid[:, :, None, None], picked, jnp.zeros_like(picked))


def projections(factor_rows, masked):
    proj_i = jnp.einsum(
        "tavn,tabvr->tabrn", factor_rows[:, :4], masked, preferred_element_type=jnp.float32
    )
    proj_j = jnp.einsum(
        "tbvn,tabvr->tabrn", factor_rows[:, 4:], masked, preferred_element_type=jnp.float32
    )
    return (proj_i.astype(jnp.bfloat16), proj_j.astype(jnp.bfloat16))


def body(
    factors,
    orbital_owner,
    tile_orbitals,
    projectors,
    amplitudes,
    ranks,
    pair_energies,
    orbital_energies,
):
    dev_count = lax.axis_size("dev")
    my_index = lax.axis_index("dev")
    tile_count = tile_orbitals.shape[0]
    orb_count = factors.shape[0]
    factor_width = factors.shape[1]
    aux_width = factors.shape[2]
    rank_width = projectors.shape[2]
    need_count = tile_count * 7
    slot_cap = -(-(8 * tile_count) // dev_count)
    my_orbitals = tile_orbitals.reshape(need_count)
    requests = lax.all_gather(my_orbitals, "dev", axis=0, tiled=True).reshape(dev_count, need_count)
    owners = orbital_owner[requests]
    entry_index = jnp.arange(need_count)
    earlier = entry_index[None, :] < entry_index[:, None]
    same_owner = owners[:, :, None] == owners[:, None, :]
    slots = jnp.sum((same_owner & earlier[None]).astype(jnp.int32), axis=2)
    owner_rows = requests // dev_count
    slot_index = jnp.arange(slot_cap)
    send_match = (owners[:, None, :] == my_index) & (slots[:, None, :] == slot_index[None, :, None])
    out_rows = jnp.sum(jnp.where(send_match, owner_rows[:, None, :], 0), axis=2)
    out_valid = jnp.any(send_match, axis=2)
    my_owner = owners[my_index]
    my_slot = slots[my_index]
    arrived = lax.all_to_all(
        pack_slots(factors, out_rows, out_valid), "dev", split_axis=0, concat_axis=0, tiled=True
    )
    fetched = arrived[my_owner, my_slot].reshape(tile_count, 7, factor_width, aux_width)
    rank_keep = jnp.arange(rank_width)[None, :] < ranks[:, None]
    masked = (projectors * rank_keep.astype(jnp.bfloat16)[:, None, :]).reshape(
        tile_count, 4, 3, factor_width, rank_width
    )
    proj_i, proj_j = projections(fetched, masked)
    amp_half = amplitudes.astype(jnp.bfloat16).reshape(tile_count, 4, 3, rank_width, rank_width)
    cycle_i = jnp.einsum(
        "tabrc,tabcn->tabrn", amp_half, proj_j, preferred_element_type=jnp.float32
    ).astype(jnp.bfloat16)
    cycle_j = jnp.einsum(
        "tabrc,tabrn->tabcn", amp_half, proj_i, preferred_element_type=jnp.float32
    ).astype(jnp.bfloat16)
    sum_i = jnp.einsum("tabvr,tabrn->tavn", masked, cycle_i, preferred_element_type=jnp.float32)
    sum_j = jnp.einsum("tabvr,tabrn->tbvn", masked, cycle_j, preferred_element_type=jnp.float32)
    partial_value = (
        jnp.concatenate([sum_i, sum_j], axis=1)
        .astype(jnp.bfloat16)
        .reshape(need_count, factor_width, aux_width)
    )
    peer_index = jnp.arange(dev_count)
    back_match = (my_owner[None, None, :] == peer_index[:, None, None]) & (
        my_slot[None, None, :] == slot_index[None, :, None]
    )
    back_index = jnp.sum(jnp.where(back_match, entry_index[None, None, :], 0), axis=2)
    back_valid = jnp.any(back_match, axis=2)
    outgoing = pack_slots(partial_value, back_index, back_valid)
    selector = (
        (out_rows.reshape(-1)[None, :] == jnp.arange(orb_count)[:, None])
        & out_valid.reshape(-1)[None, :]
    ).astype(jnp.bfloat16)
    incoming = lax.all_to_all(outgoing, "dev", split_axis=0, concat_axis=0, tiled=True)
    totals = jnp.einsum(
        "mq,qvn->mvn",
        selector,
        incoming.reshape(dev_count * slot_cap, factor_width, aux_width),
        preferred_element_type=jnp.float32,
    )
    orbital_sums = totals.astype(jnp.bfloat16)
    returned = lax.all_to_all(
        pack_slots(orbital_sums, out_rows, out_valid),
        "dev",
        split_axis=0,
        concat_axis=0,
        tiled=True,
    )
    collected = returned[my_owner, my_slot].reshape(tile_count, 7, factor_width, aux_width)
    corr_i, corr_j = projections(collected, masked)
    residual = jnp.einsum("tabrn,tabcn->tabrc", proj_i, proj_j, preferred_element_type=jnp.float32)
    residual = residual + jnp.einsum(
        "tabrn,tabcn->tabrc", proj_i, corr_j, preferred_element_type=jnp.float32
    )
    residual = residual + jnp.einsum(
        "tabrn,tabcn->tabrc", corr_i, proj_j, preferred_element_type=jnp.float32
    )
    energy = pair_energies.reshape(tile_count, 4, 3, rank_width)
    occ_gaps = orbital_energies[my_orbitals].reshape(tile_count, 7)
    denominator = energy[:, :, :, :, None] + energy[:, :, :, None, :]
    denominator = (
        denominator + occ_gaps[:, :4, None, None, None] + occ_gaps[:, None, 4:, None, None]
    )
    keep_float = rank_keep.astype(jnp.float32).reshape(tile_count, 4, 3, rank_width)
    updated = (
        -(keep_float[:, :, :, :, None] * keep_float[:, :, :, None, :]) * residual / denominator
    )
    return (updated.reshape(tile_count * 12, rank_width, rank_width), orbital_sums)


def solution(mesh):
    in_specs = (
        P("dev", None, None),
        P(),
        P("dev", None),
        P("dev", None, None),
        P("dev", None, None),
        P("dev"),
        P("dev", None),
        P(),
    )
    out_specs = (P("dev", None, None), P("dev", None, None))
    return jax.shard_map(body, mesh=mesh, in_specs=in_specs, out_specs=out_specs, check_vma=False)
```

profile of v0, /device:TPU:1, one launch (start us, length us, event | category | flops | bytes accessed | tf_op | source)
XLA Modules:
  0.0 604.1 jit_solution(10534735102988396978)
XLA Ops:
  0.7 0.8 reshape.388
  1.5 0.3 dynamic-update-slice
  1.8 40.5 %all-reduce = s32[1792]{0:T(1024)S(1)} all-reduce(s32[1792]{0:T(1024)S(1)} %dynamic-update-slice), channel_id=1, replica_groups=mesh['dev'=32] {'dev'}, use_global_device_ids=true, to_apply=%add | all-reduce | flops 1792 | bytes 14336
  42.5 0.1 reshape.334
  42.6 10.9 %gather_fusion = s32[1792]{0:T(1024)S(1)} fusion(s32[256]{0:T(256)S(1)} %copy-done.2, s32[2048]{0:T(1024)S(1)} %pad_clamp_fusion), kind=kCustom, calls=%fused_computation | custom fusion | bytes 21504 | tf_op jit(solution)/shard_map/gather | solution.py:43
  53.6 0.9 convert_reduce_fusion
  54.5 0.1 fusion.63
  54.7 0.1 select_reduce_fusion
  54.8 0.1 copy.31
  54.9 0.1 reshape.342
  55.0 0.1 copy.30
  55.1 3.7 gather_fusion.1
  58.8 6.0 broadcast_select_fusion.2
  64.7 5.7 all-to-all-start
  70.5 5.1 convert_element_type.69
  75.6 0.1 fusion.61
  75.8 0.1 copy.43
  75.8 0.1 reshape.356
  76.0 0.1 and_reduce_fusion
  76.1 0.1 copy.36
  76.3 4.8 broadcast_multiply_fusion
  81.1 128.5 %all-to-all-done = bf16[32,2,192,256]{3,2,1,0:T(8,128)(2,1)} async-done(((bf16[32,2,192,256]{3,2,1,0:T(8,128)(2,1)}), bf16[32,2,192,256]{3,2,1,0:T(8,128)(2,1)}, u32[]{:S(2)}, u32[]{:S(2)}) %all-to-all-start) | async-done | bytes 6291488 | tf_op jit(solution)/shard_map/all_to_all | solution.py:55
  209.7 6.2 %gather_fusion.2 = bf16[56,192,256]{2,1,0:T(8,128)(2,1)} fusion(bf16[32,2,192,256]{3,2,1,0:T(8,128)(2,1)} %all-to-all-done, s32[56]{0:T(128)S(1)} %fusion.77), kind=kCustom, calls=%fused_computation.2 | custom fusion | bytes 11010496 | tf_op jit(solution)/shard_map/gather | solution.py:58
  215.9 7.8 %convert_bitcast_fusion = bf16[8,4,3,128,256]{4,3,1,2,0:T(8,128)(2,1)} fusion(bf16[8,4,3,192,128]{4,3,2,1,0:T(8,128)(2,1)} %bitcast.90, bf16[8,7,192,256]{3,2,1,0:T(8,128)(2,1)} %bitcast.102), kind=kOutput, calls=%fused_computation.24 | convolution fusion | flops 1211105280 | bytes 13369344 | tf_op jit(solution)/shard_map/tbvn,tabvr->tabrn/dot_general | solution.py:16
  223.7 6.4 %convolution_convert_fusion = bf16[8,4,3,128,256]{4,3,2,1,0:T(8,128)(2,1)} fusion(bf16[8,4,3,192,128]{4,3,2,1,0:T(8,128)(2,1)S(1)} %bitcast.97, bf16[8,7,192,256]{3,2,1,0:T(8,128)(2,1)} %bitcast.103), kind=kOutput, calls=%fused_computation.40 | convolution fusion | flops 1211105280 | bytes 14155776 | tf_op jit(solution)/shard_map/tavn,tabvr->tabrn/dot_general | solution.py:13
  230.2 8.5 %bitcast_convert_fusion = bf16[8,4,192,256]{3,2,1,0:T(8,128)(2,1)} fusion(bf16[8,4,3,192,128]{4,3,2,1,0:T(8,128)(2,1)} %bitcast.91, bf16[8,4,3,128,128]{4,3,2,1,0:T(8,128)(2,1)} %bitcast.106, bf16[8,4,3,128,256]{4,3,1,2,0:T(8,128)(2,1)} %convert_bitcast_fusion), kind=kOutput, calls=%fused_computation.15 | convolution fusion | flops 2017984512 | bytes 17301504 | tf_op jit(solution)/shard_map/tabvr,tabrn->tavn/dot_general | solution.py:71
  238.7 8.9 %bitcast_convert_fusion.1 = bf16[8,3,192,256]{3,2,1,0:T(8,128)(2,1)} fusion(bf16[8,4,3,128,128]{4,3,2,1,0:T(8,128)(2,1)} %bitcast.107, bf16[8,4,3,128,256]{4,3,2,1,0:T(8,128)(2,1)} %convolution_convert_fusion, bf16[8,4,3,192,128]{4,3,2,1,0:T(8,128)(2,1)} %bitcast.92), kind=kOutput, calls=%fused_computation.34 | convolution fusion | flops 2017591296 | bytes 16515072 | tf_op jit(solution)/shard_map/tabvr,tabrn->tbvn/dot_general | solution.py:72
  247.6 5.4 pad_maximum_fusion
  253.0 6.2 %gather_fusion.3 = bf16[64,192,256]{2,1,0:T(8,128)(2,1)} fusion(bf16[56,192,256]{2,1,0:T(8,128)(2,1)} %bitcast.98, s32[1024]{0:T(1024)S(1)} %pad_clamp_fusion.2), kind=kCustom, calls=%fused_computation.3 | custom fusion | bytes 12583168 | tf_op jit(solution)/shard_map/gather | solution.py:8
  259.2 6.0 broadcast_select_fusion
  265.2 4.1 all-to-all-start.1
  269.3 0.1 copy.34
  269.4 0.1 and.58
  269.5 0.1 eq.98
  269.6 139.0 %all-to-all-done.1 = bf16[32,2,192,256]{3,2,1,0:T(8,128)(2,1)} async-done(((bf16[32,2,192,256]{3,2,1,0:T(8,128)(2,1)}), bf16[32,2,192,256]{3,2,1,0:T(8,128)(2,1)}, u32[]{:S(2)}, u32[]{:S(2)}) %all-to-all-start.1) | async-done | bytes 6291488 | tf_op jit(solution)/shard_map/all_to_all | solution.py:89
  408.7 6.2 %fusion.54 = bf16[8,192,256]{2,0,1:T(8,128)(2,1)S(1)} fusion(bf16[64,192,256]{2,1,0:T(8,128)(2,1)} %bitcast.25, s32[64]{0:T(128)S(1)} %eq.98, pred[64]{0:T(512)(128)(4,1)S(1)} %and.58), kind=kOutput, calls=%fused_computation.47 | convolution fusion | flops 50725888 | bytes 7078208 | tf_op jit(solution)/shard_map/mq,qvn->mvn/dot_general | solution.py:90
  414.9 0.2 copy.45
  415.0 3.7 gather_fusion.4
  418.7 6.0 broadcast_select_fusion.1
  424.7 4.2 all-to-all-start.2
  429.0 0.1 lt.121
  429.2 0.8 gather_fusion.6
  430.2 0.1 fusion.59
  430.3 137.9 %all-to-all-done.2 = bf16[32,2,192,256]{3,2,1,0:T(8,128)(2,1)} async-done(((bf16[32,2,192,256]{3,2,1,0:T(8,128)(2,1)}), bf16[32,2,192,256]{3,2,1,0:T(8,128)(2,1)}, u32[]{:S(2)}, u32[]{:S(2)}) %all-to-all-start.2) | async-done | bytes 6291488 | tf_op jit(solution)/shard_map/all_to_all | solution.py:97
  568.2 6.1 %gather_fusion.5 = bf16[56,192,256]{2,1,0:T(8,128)(2,1)} fusion(bf16[32,2,192,256]{3,2,1,0:T(8,128)(2,1)} %all-to-all-done.2, s32[56]{0:T(128)S(1)} %fusion.77), kind=kCustom, calls=%fused_computation.5 | custom fusion | bytes 11010496 | tf_op jit(solution)/shard_map/gather | solution.py:104
  574.3 8.5 %fusion = f32[8,4,3,128,128]{4,3,2,1,0:T(8,128)} fusion(bf16[8,4,3,128,256]{4,3,2,1,0:T(8,128)(2,1)} %convolution_convert_fusion, bf16[8,4,3,192,128]{4,3,2,1,0:T(8,128)(2,1)} %bitcast.93, bf16[8,7,192,256]{3,2,1,0:T(8,128)(2,1)} %bitcast.104), kind=kOutput, calls=%fused_computation.7 | convolution fusion | flops 2016411648 | bytes 19660800 | tf_op jit(solution)/shard_map/tabrn,tabcn->tabrc/dot_general | solution.py:107
  582.8 8.7 %fusion.10 = f32[8,4,3,128,128]{4,3,2,1,0:T(8,128)} fusion(bf16[8,4,3,128,256]{4,3,1,2,0:T(8,128)(2,1)} %convert_bitcast_fusion, bf16[8,4,3,192,128]{4,3,2,1,0:T(8,128)(2,1)} %bitcast.94, bf16[8,7,192,256]{3,2,1,0:T(8,128)(2,1)} %bitcast.105), kind=kOutput, calls=%fused_computation.19 | convolution fusion | flops 2016411648 | bytes 20447232 | tf_op jit(solution)/shard_map/tabrn,tabcn->tabrc/dot_general | solution.py:110
  591.5 12.6 %add_divide_fusion = f32[8,4,3,128,128]{4,3,2,1,0:T(8,128)} fusion(f32[8,4,3,128,128]{4,3,2,1,0:T(8,128)} %fusion.10, f32[8,4,3,128,128]{4,3,2,1,0:T(8,128)} %fusion, f32[8,3]{1,0:T(8,128)S(1)} %slice.23, f32[8,4]{1,0:T(8,128)S(1)} %bitcast.108, f32[8,4,3,128]{3,2,1,0:T(4,128)S(1)} %add.128, f32[8,4,3,128]{3,2,1,0:T(4,128)S(1)} %fusion.59, ...), kind=kOutput, calls=%fused_computation.18 | convolution fusion | flops 819462144 | bytes 31555808 | tf_op jit(solution)/shard_map/tabrn,tabcn->tabrc/dot_general | solution.py:106
  (45 shorter events, 0.7 us)
Async XLA Ops:
  0.6 54.5 %copy-start = (bf16[8,192,256]{2,1,0:T(8,128)(2,1)S(1)}, bf16[8,192,256]{2,1,0:T(8,128)(2,1)}, u32[]{:S(2)}) copy-start(bf16[8,192,256]{2,1,0:T(8,128)(2,1)} %param.8) | copy-start | bytes 2359300
  0.6 41.9 %copy-start.2 = (s32[256]{0:T(256)S(1)}, s32[256]{0:T(256)}, u32[]{:S(2)}) copy-start(s32[256]{0:T(256)} %param.9) | copy-start | bytes 3076
  64.7 144.9 %all-to-all-start = ((bf16[32,2,192,256]{3,2,1,0:T(8,128)(2,1)}), bf16[32,2,192,256]{3,2,1,0:T(8,128)(2,1)}, u32[]{:S(2)}, u32[]{:S(2)}) async-start(bf16[32,2,192,256]{3,2,1,0:T(8,128)(2,1)} %broadcast_select_fusion.2), calls=%async_computation | async-start | bytes 12582912 | tf_op jit(solution)/shard_map/all_to_all | solution.py:55
  70.4 5.8 copy-start.7
  209.7 14.1 %slice-start = ((s8[4718592]{0:T(1024)(128)(4,1)}), s8[524288]{0:T(1024)(128)(4,1)S(1)}, s32[]{:S(2)}) async-start(s8[4718592]{0:T(1024)(128)(4,1)} %bitcast.95), calls=%async_computation.3 | async-start | bytes 1048576
  215.9 7.8 %slice-start.1 = ((s8[4718592]{0:T(1024)(128)(4,1)}), s8[4194304]{0:T(1024)(128)(4,1)S(1)}, s32[]{:S(2)}) async-start(s8[4718592]{0:T(1024)(128)(4,1)} %bitcast.95), calls=%async_computation.4 | async-start | bytes 8388608
  265.2 143.5 %all-to-all-start.1 = ((bf16[32,2,192,256]{3,2,1,0:T(8,128)(2,1)}), bf16[32,2,192,256]{3,2,1,0:T(8,128)(2,1)}, u32[]{:S(2)}, u32[]{:S(2)}) async-start(bf16[32,2,192,256]{3,2,1,0:T(8,128)(2,1)} %broadcast_select_fusion), calls=%async_computation.1 | async-start | bytes 12582912 | tf_op jit(solution)/shard_map/all_to_all | solution.py:89
  415.0 3.7 copy-start.4
  424.7 4.3 copy-start.6
  424.7 4.5 copy-start.3
  424.7 5.4 copy-start.5
  424.7 143.5 %all-to-all-start.2 = ((bf16[32,2,192,256]{3,2,1,0:T(8,128)(2,1)}), bf16[32,2,192,256]{3,2,1,0:T(8,128)(2,1)}, u32[]{:S(2)}, u32[]{:S(2)}) async-start(bf16[32,2,192,256]{3,2,1,0:T(8,128)(2,1)} %broadcast_select_fusion.1), calls=%async_computation.2 | async-start | bytes 12582912 | tf_op jit(solution)/shard_map/all_to_all | solution.py:97
  591.5 12.6 %copy-start.1 = (bf16[8,192,256]{2,1,0:T(8,128)(2,1)S(1)}, bf16[8,192,256]{2,1,0:T(8,128)(2,1)}, u32[]{:S(2)}) copy-start(bf16[8,192,256]{2,1,0:T(8,128)(2,1)} %param.8) | copy-start | bytes 2359300
where the time goes:
time: 606 us; the launch traced here: 604 us
  waiting for transfers between devices  405 us (67%)
  matrix products  67.6 us (11%)
  local copies, waits for them, and re-layouts  40.5 us (7%)
  blocking collectives  40.5 us (7%)
  other arithmetic  34.9 us (6%)
  starting transfers between devices  14.1 us (2%)
    all_to_all x1, waiting for transfers between devices, body(): lax.all_to_all(outgoing, 'dev', split_axis=0, concat_axis=0, tiled=True)  139 us
    all_to_all x1, waiting for transfers between devices, body(): lax.all_to_all(pack_slots(orbital_sums, out_rows, out_valid), 'dev', spli...  138 us
    all_to_all x1, waiting for transfers between devices, body(): lax.all_to_all(pack_slots(factors, out_rows, out_valid), 'dev', split_axi...  129 us
    unnamed x1, blocking collectives  40.5 us
    select_n x3, other arithmetic, pack_slots(): jnp.where(slot_valid[:, :, None, None], picked, jnp.zeros_like(picked))  17.9 us
    gather x3, local copies, waits for them, and re-layouts, pack_slots(): picked = source_table[slot_rows]  13.5 us
    dot_general x1, matrix products, body(): jnp.einsum('tabrn,tabcn->tabrc', proj_i, proj_j, preferred_element_type=j...  12.6 us
  transfers between devices with their start and end apart: 3, of which 3 were waited for; matrix products, arithmetic and copies ran while one was open for 2% of the time, Pallas kernels for 0%

commit v1 on v0

--- a/solution.py
+++ b/solution.py
@@ -19,7 +19,10 @@
     return (proj_i.astype(jnp.bfloat16), proj_j.astype(jnp.bfloat16))
 
 
-def body(
+GATHER_BYTES = 40 << 20
+
+
+def slot_body(
     factors,
     orbital_owner,
     tile_orbitals,
@@ -123,6 +126,82 @@
     return (updated.reshape(tile_count * 12, rank_width, rank_width), orbital_sums)
 
 
+def gather_body(
+    factors,
+    orbital_owner,
+    tile_orbitals,
+    projectors,
+    amplitudes,
+    ranks,
+    pair_energies,
+    orbital_energies,
+):
+    dev_count = lax.axis_size("dev")
+    tile_count = tile_orbitals.shape[0]
+    factor_width = factors.shape[1]
+    aux_width = factors.shape[2]
+    orb_count = factors.shape[0]
+    rank_width = projectors.shape[2]
+    need_count = tile_count * 7
+    my_orbitals = tile_orbitals.reshape(need_count)
+    rows = orbital_owner[my_orbitals] * orb_count + my_orbitals // dev_count
+    all_factors = lax.all_gather(factors, "dev", axis=0, tiled=True)
+    fetched = all_factors[rows].reshape(tile_count, 7, factor_width, aux_width)
+    rank_keep = jnp.arange(rank_width)[None, :] < ranks[:, None]
+    masked = (projectors * rank_keep.astype(jnp.bfloat16)[:, None, :]).reshape(
+        tile_count, 4, 3, factor_width, rank_width
+    )
+    proj_i, proj_j = projections(fetched, masked)
+    amp_half = amplitudes.astype(jnp.bfloat16).reshape(tile_count, 4, 3, rank_width, rank_width)
+    cycle_i = jnp.einsum(
+        "tabrc,tabcn->tabrn", amp_half, proj_j, preferred_element_type=jnp.float32
+    ).astype(jnp.bfloat16)
+    cycle_j = jnp.einsum(
+        "tabrc,tabrn->tabcn", amp_half, proj_i, preferred_element_type=jnp.float32
+    ).astype(jnp.bfloat16)
+    sum_i = jnp.einsum("tabvr,tabrn->tavn", masked, cycle_i, preferred_element_type=jnp.float32)
+    sum_j = jnp.einsum("tabvr,tabrn->tbvn", masked, cycle_j, preferred_element_type=jnp.float32)
+    partial_value = (
+        jnp.concatenate([sum_i, sum_j], axis=1)
+        .astype(jnp.bfloat16)
+        .reshape(need_count, factor_width, aux_width)
+    )
+    total_rows = dev_count * orb_count
+    hit = rows[None, :] == jnp.arange(total_rows)[:, None]
+    where_from = jnp.sum(jnp.where(hit, jnp.arange(need_count)[None, :], 0), axis=1)
+    named = jnp.any(hit, axis=1)
+    dense = jnp.where(
+        named[:, None, None], partial_value[where_from], jnp.zeros((), jnp.bfloat16)
+    )
+    orbital_sums = lax.psum_scatter(dense, "dev", scatter_dimension=0, tiled=True)
+    all_sums = lax.all_gather(orbital_sums, "dev", axis=0, tiled=True)
+    collected = all_sums[rows].reshape(tile_count, 7, factor_width, aux_width)
+    corr_i, corr_j = projections(collected, masked)
+    residual = jnp.einsum("tabrn,tabcn->tabrc", proj_i, proj_j, preferred_element_type=jnp.float32)
+    residual = residual + jnp.einsum(
+        "tabrn,tabcn->tabrc", proj_i, corr_j, preferred_element_type=jnp.float32
+    )
+    residual = residual + jnp.einsum(
+        "tabrn,tabcn->tabrc", corr_i, proj_j, preferred_element_type=jnp.float32
+    )
+    energy = pair_energies.reshape(tile_count, 4, 3, rank_width)
+    occ_gaps = orbital_energies[my_orbitals].reshape(tile_count, 7)
+    denominator = energy[:, :, :, :, None] + energy[:, :, :, None, :]
+    denominator = (
+        denominator + occ_gaps[:, :4, None, None, None] + occ_gaps[:, None, 4:, None, None]
+    )
+    keep_float = rank_keep.astype(jnp.float32).reshape(tile_count, 4, 3, rank_width)
+    updated = (
+        -(keep_float[:, :, :, :, None] * keep_float[:, :, :, None, :]) * residual / denominator
+    )
+    return (updated.reshape(tile_count * 12, rank_width, rank_width), orbital_sums)
+
+
+def body(factors, *rest):
+    gathered = lax.axis_size("dev") * factors.size * factors.dtype.itemsize
+    return (gather_body if gathered <= GATHER_BYTES else slot_body)(factors, *rest)
+
+
 def solution(mesh):
     in_specs = (
         P("dev", None, None),

time: 606 us -> 700 us (1.16)
  waiting for transfers between devices: 405 us -> 545 us
  blocking collectives: 40.5 us -> 0 us
  starting transfers between devices: 14.1 us -> 0.12 us
  between operations: 0.93 us -> 13.8 us
    all_to_all x3 -> x0, waiting for transfers between devices: 405 us -> none  [the longest x1 139 us: body(): lax.all_to_all(outgoing, 'dev', split_axis=0, concat_axis=0, tiled=True)]
    all_gather x0 -> x2, waiting for transfers between devices: none -> 303 us  [the longest x1 157 us: gather_body(): all_sums = lax.all_gather(orbital_sums, 'dev', axis=0, tiled=True)]
    reduce_scatter x0 -> x1, waiting for transfers between devices: none -> 240 us  [gather_body(): lax.psum_scatter(dense, 'dev', scatter_dimension=0, tiled=True)]
    unnamed x1 -> x0, blocking collectives: 40.5 us -> none
    all_to_all x3 -> x0, starting transfers between devices: 14.1 us -> none  [the longest x1 5.71 us: body(): lax.all_to_all(pack_slots(factors, out_rows, out_valid), 'dev', split_axi...]
    dot_general x6 -> x5, matrix products: 53.3 us -> 47.9 us  [the longest x1 12.5 us: gather_body(): jnp.einsum('tabrn,tabcn->tabrc', proj_i, proj_j, preferred_element_type=j...]
    select_n x8 -> x4, other arithmetic: 18 us -> 21.6 us  [the longest x1 21.6 us: gather_body(): jnp.where(named[:, None, None], partial_value[where_from], jnp.zeros((),...]
    gather x8 -> x5, local copies, waits for them, and re-layouts: 37.7 us -> 39.1 us  [the longest x1 14.4 us: gather_body(): partial_value[where_from]]
where the time goes in v1:
time: 700 us; the launch traced here: 699 us
  waiting for transfers between devices  545 us (78%)
  matrix products  62.3 us (9%)
  local copies, waits for them, and re-layouts  40.9 us (6%)
  other arithmetic  37.5 us (5%)
  between operations  13.8 us (2%)
    reduce_scatter x1, waiting for transfers between devices, gather_body(): lax.psum_scatter(dense, 'dev', scatter_dimension=0, tiled=True)  240 us
    all_gather x1, waiting for transfers between devices, gather_body(): all_sums = lax.all_gather(orbital_sums, 'dev', axis=0, tiled=True)  157 us
    all_gather x1, waiting for transfers between devices, gather_body(): all_factors = lax.all_gather(factors, 'dev', axis=0, tiled=True)  147 us
    select_n x1, other arithmetic, gather_body(): jnp.where(named[:, None, None], partial_value[where_from], jnp.zeros((),...  21.6 us
    gather x1, local copies, waits for them, and re-layouts, gather_body(): partial_value[where_from]  14.4 us
  transfers between devices with their start and end apart: 3, of which 3 were waited for; matrix products, arithmetic and copies ran while one was open for 2% of the time, Pallas kernels for 0%

profile of v1, /device:TPU:1, one launch (start us, length us, event | category | flops | bytes accessed | tf_op | source)
XLA Modules:
  0.0 699.3 jit_solution(14186606163208614713)
XLA Ops:
  7.2 0.0 copy-start
  7.2 0.0 copy-start.5
  7.2 0.0 all-gather.3.cloned.1.call-start
  7.2 0.7 all-gather.3.cloned.1.call-update
  7.9 0.0 reduce-scatter.2.cloned.1.call-start
  8.0 0.8 reshape.237
  8.7 0.8 reshape.239
  9.5 5.1 convert_element_type.61
  14.6 0.0 copy-done
  14.6 0.8 gather_fusion
  15.5 0.1 select_reduce_fusion
  15.6 0.1 fusion.55
  15.7 0.0 copy-done.5
  15.7 0.1 fusion.56
  15.8 4.9 broadcast_multiply_fusion
  20.7 146.8 %all-gather.3.cloned.1.call-done = bf16[256,192,256]{2,1,0:T(8,128)(2,1)} async-done(((bf16[8,192,256]{2,1,0:T(8,128)(2,1)}), bf16[256,192,256]{2,1,0:T(8,128)(2,1)}) %all-gather.3.cloned.1.call-update) | async-done | bytes 25165840 | tf_op jit(solution)/shard_map/all_gather | solution.py:148
  167.4 0.0 slice-start
  167.4 11.6 %gather_fusion.1 = bf16[56,192,256]{2,1,0:T(8,128)(2,1)} fusion(bf16[256,192,256]{2,1,0:T(8,128)(2,1)} %all-gather.3.cloned.1.call-done, s32[1024]{0:T(1024)S(1)} %pad_clamp_fusion.1), kind=kCustom, calls=%fused_computation.1 | custom fusion | bytes 11010272 | tf_op jit(solution)/shard_map/gather | solution.py:149
  179.0 0.0 slice-start.1
  179.0 7.9 %convert_bitcast_fusion = bf16[8,4,3,128,256]{4,3,1,2,0:T(8,128)(2,1)} fusion(bf16[8,4,3,192,128]{4,3,2,1,0:T(8,128)(2,1)} %bitcast.68, bf16[8,7,192,256]{3,2,1,0:T(8,128)(2,1)} %bitcast.76), kind=kOutput, calls=%fused_computation.21 | convolution fusion | flops 1211105280 | bytes 13369344 | tf_op jit(solution)/shard_map/tbvn,tabvr->tabrn/dot_general | solution.py:16
  186.9 0.0 slice-done
  186.9 0.0 slice-done.1
  186.9 6.5 convolution_convert_fusion
  193.4 0.0 copy-start.3
  193.5 10.4 %bitcast_convert_fusion = bf16[8,4,192,256]{3,2,1,0:T(8,128)(2,1)} fusion(bf16[8,4,3,192,128]{4,3,2,1,0:T(8,128)(2,1)} %bitcast.69, bf16[8,4,3,128,128]{4,3,2,1,0:T(8,128)(2,1)} %bitcast.80, bf16[8,4,3,128,256]{4,3,1,2,0:T(8,128)(2,1)} %convert_bitcast_fusion), kind=kOutput, calls=%fused_computation.12 | convolution fusion | flops 2017984512 | bytes 17301504 | tf_op jit(solution)/shard_map/tabvr,tabrn->tavn/dot_general | solution.py:162
  203.8 0.0 copy-done.3
  203.8 7.8 %bitcast_convert_fusion.1 = bf16[8,3,192,256]{3,2,1,0:T(8,128)(2,1)} fusion(bf16[8,4,3,128,128]{4,3,2,1,0:T(8,128)(2,1)S(1)} %bitcast.81, bf16[8,4,3,128,256]{4,3,2,1,0:T(8,128)(2,1)} %convolution_convert_fusion, bf16[8,4,3,192,128]{4,3,2,1,0:T(8,128)(2,1)} %bitcast.70), kind=kOutput, calls=%fused_computation.28 | convolution fusion | flops 2017591296 | bytes 16515072 | tf_op jit(solution)/shard_map/tabvr,tabrn->tbvn/dot_general | solution.py:163
  211.6 5.5 pad_maximum_fusion
  217.2 14.4 %gather_fusion.2 = bf16[256,192,256]{2,1,0:T(8,128)(2,1)} fusion(bf16[56,192,256]{2,1,0:T(8,128)(2,1)} %bitcast.67, s32[1024]{0:T(1024)S(1)} %pad_clamp_fusion), kind=kCustom, calls=%fused_computation.2 | custom fusion | bytes 50332672 | tf_op jit(solution)/shard_map/gather | solution.py:174
  231.5 21.6 %broadcast_select_fusion = bf16[256,192,256]{2,1,0:T(8,128)(2,1)} fusion(bf16[256,192,256]{2,1,0:T(8,128)(2,1)} %gather_fusion.2, pred[256]{0:T(512)(128)(4,1)S(1)} %fusion.55), kind=kLoop, calls=%fused_computation.5 | loop fusion | flops 12582912 | bytes 50331904 | tf_op jit(solution)/shard_map/jit(_where)/select_n | solution.py:173
  253.1 0.0 copy-start.2
  253.1 0.0 reduce-scatter.2.cloned.1.call-update
  253.1 0.0 all-gather.5.cloned.1.call-start
  253.2 240.5 %reduce-scatter.2.cloned.1.call-done = bf16[8,192,256]{2,1,0:T(8,128)(2,1)} async-done(((bf16[256,192,256]{2,1,0:T(8,128)(2,1)}), bf16[8,192,256]{2,1,0:T(8,128)(2,1)}) %reduce-scatter.2.cloned.1.call-update) | async-done | bytes 786448 | tf_op jit(solution)/shard_map/reduce_scatter | solution.py:176
  493.6 0.0 all-gather.5.cloned.1.call-update
  493.7 0.1 lt.72
  493.8 0.0 copy-done.2
  493.8 0.8 gather_fusion.4
  494.6 0.1 reshape.242
  494.7 0.1 slice.23
  494.7 0.0 copy-done.4
  494.8 0.1 fusion.54
  494.9 156.7 %all-gather.5.cloned.1.call-done = bf16[256,192,256]{2,1,0:T(8,128)(2,1)} async-done(((bf16[8,192,256]{2,1,0:T(8,128)(2,1)}), bf16[256,192,256]{2,1,0:T(8,128)(2,1)}) %all-gather.5.cloned.1.call-update) | async-done | bytes 25165840 | tf_op jit(solution)/shard_map/all_gather | solution.py:177
  651.6 11.5 %gather_fusion.3 = bf16[56,192,256]{2,1,0:T(8,128)(2,1)} fusion(bf16[256,192,256]{2,1,0:T(8,128)(2,1)} %all-gather.5.cloned.1.call-done, s32[1024]{0:T(1024)S(1)} %pad_clamp_fusion.1), kind=kCustom, calls=%fused_computation.3 | custom fusion | bytes 11010272 | tf_op jit(solution)/shard_map/gather | solution.py:178
  663.1 8.5 %fusion = f32[8,4,3,128,128]{4,3,2,1,0:T(8,128)} fusion(bf16[8,4,3,128,256]{4,3,2,1,0:T(8,128)(2,1)} %convolution_convert_fusion, bf16[8,4,3,192,128]{4,3,2,1,0:T(8,128)(2,1)} %bitcast.71, bf16[8,7,192,256]{3,2,1,0:T(8,128)(2,1)} %bitcast.78), kind=kOutput, calls=%fused_computation.6 | convolution fusion | flops 2016411648 | bytes 19660800 | tf_op jit(solution)/shard_map/tabrn,tabcn->tabrc/dot_general | solution.py:181
  671.5 8.7 %fusion.8 = f32[8,4,3,128,128]{4,3,2,1,0:T(8,128)} fusion(bf16[8,4,3,128,256]{4,3,1,2,0:T(8,128)(2,1)} %convert_bitcast_fusion, bf16[8,4,3,192,128]{4,3,2,1,0:T(8,128)(2,1)} %bitcast.72, bf16[8,7,192,256]{3,2,1,0:T(8,128)(2,1)} %bitcast.79), kind=kOutput, calls=%fused_computation.16 | convolution fusion | flops 2016411648 | bytes 20447232 | tf_op jit(solution)/shard_map/tabrn,tabcn->tabrc/dot_general | solution.py:184
  680.2 12.5 %add_divide_fusion = f32[8,4,3,128,128]{4,3,2,1,0:T(8,128)} fusion(f32[8,4,3,128,128]{4,3,2,1,0:T(8,128)} %fusion.8, f32[8,4,3,128,128]{4,3,2,1,0:T(8,128)} %fusion, f32[8,3]{1,0:T(8,128)S(1)} %slice.23, f32[8,4]{1,0:T(8,128)S(1)} %bitcast.82, f32[8,4,3,128]{3,2,1,0:T(4,128)S(1)} %add.110, f32[8,4,3,128]{3,2,1,0:T(4,128)S(1)} %fusion.54, ...), kind=kOutput, calls=%fused_computation.15 | convolution fusion | flops 819462144 | bytes 31555808 | tf_op jit(solution)/shard_map/tabrn,tabcn->tabrc/dot_general | solution.py:180
  692.8 0.0 copy-done.1
  (11 shorter events, 0.1 us)
Async XLA Ops:
  7.2 7.5 %copy-start = (s32[256]{0:T(256)S(1)}, s32[256]{0:T(256)}, u32[]{:S(2)}) copy-start(s32[256]{0:T(256)} %param.9) | copy-start | bytes 3076
  7.2 8.5 %copy-start.5 = (s32[96]{0:T(128)S(1)}, s32[96]{0:T(128)}, u32[]{:S(2)}) copy-start(s32[96]{0:T(128)} %param.13) | copy-start | bytes 1156
  7.2 160.2 %all-gather.3.cloned.1.call-start = ((), (), s32[]{:S(2)}) async-start(), calls=%async_computation.1 | async-start | bytes 25952256 | tf_op jit(solution)/shard_map/all_gather | solution.py:148
  7.9 485.7 %reduce-scatter.2.cloned.1.call-start = ((), (), s32[]{:S(2)}) async-start(), calls=%async_computation.2 | async-start | bytes 25952256 | tf_op jit(solution)/shard_map/reduce_scatter | solution.py:176
  167.4 19.5 %slice-start = ((s8[4718592]{0:T(1024)(128)(4,1)}), s8[524288]{0:T(1024)(128)(4,1)S(1)}, s32[]{:S(2)}) async-start(s8[4718592]{0:T(1024)(128)(4,1)} %bitcast.73), calls=%async_computation.4 | async-start | bytes 1048576
  179.0 7.9 %slice-start.1 = ((s8[4718592]{0:T(1024)(128)(4,1)}), s8[4194304]{0:T(1024)(128)(4,1)S(1)}, s32[]{:S(2)}) async-start(s8[4718592]{0:T(1024)(128)(4,1)} %bitcast.73), calls=%async_computation.5 | async-start | bytes 8388608
  193.4 10.4 %copy-start.3 = (bf16[96,128,128]{2,1,0:T(8,128)(2,1)S(1)}, bf16[96,128,128]{2,1,0:T(8,128)(2,1)}, u32[]{:S(2)}) copy-start(bf16[96,128,128]{2,1,0:T(8,128)(2,1)} %convert_element_type.61) | copy-start | bytes 9437188
  253.1 240.7 %copy-start.2 = (f32[256]{0:T(256)S(1)}, f32[256]{0:T(256)}, u32[]{:S(2)}) copy-start(f32[256]{0:T(256)} %param.15) | copy-start | bytes 3076
  253.1 241.6 %copy-start.4 = (f32[96,128]{1,0:T(8,128)S(1)}, f32[96,128]{1,0:T(8,128)}, u32[]{:S(2)}) copy-start(f32[96,128]{1,0:T(8,128)} %param.14) | copy-start | bytes 147460
  253.1 398.4 %all-gather.5.cloned.1.call-start = ((), (), s32[]{:S(2)}) async-start(), calls=%async_computation.3 | async-start | bytes 25952256 | tf_op jit(solution)/shard_map/all_gather | solution.py:177
  680.2 12.5 %copy-start.1 = (s32[256]{0:T(256)S(1)}, s32[256]{0:T(256)}, u32[]{:S(2)}) copy-start(s32[256]{0:T(256)} %param.9) | copy-start | bytes 3076
Sparse Core Ops, SparseCore 0:
  10.9 156.4 all-gather.2
  253.3 240.3 reduce-scatter.1
  497.1 154.4 all-gather.4

commit v2 on v0

v2 whole, which is shorter than its diff:
```python
import functools
import math
import jax
import jax.numpy as jnp
from jax import lax
from jax.experimental import pallas as pl
from jax.experimental.pallas import tpu as pltpu
from jax.sharding import PartitionSpec as P

PLANES = 4
MESH = pl.DeviceIdType.MESH
VMEM_LIMIT = 60 << 20


def planes_of(dev_count):
    return math.gcd(PLANES, dev_count)


def place(planes):
    width = lax.axis_size("dev") // planes
    me = lax.axis_index("dev")
    return me, lax.div(me, width), lax.rem(me, width), width


def greet(barrier, me, z, col, planes, width, lines):
    base = z * width

    @pl.loop(1, width)
    def _(step):
        peer = base + lax.rem(col + step, width)
        pl.semaphore_signal(barrier, inc=1, device_id=(peer,), device_id_type=MESH)

    count = width - 1
    if lines:

        @pl.when(z > 0)
        def _():
            pl.semaphore_signal(barrier, inc=1, device_id=(me - width,), device_id_type=MESH)

        @pl.when(z < planes - 1)
        def _():
            pl.semaphore_signal(barrier, inc=1, device_id=(me + width,), device_id_type=MESH)

        count = count + jnp.where(z > 0, 1, 0) + jnp.where(z < planes - 1, 1, 0)

    pl.semaphore_wait(barrier, count)


def ask_kernel(planes, want, got, send, recv):
    me, z, col, width = place(planes)
    greet(pltpu.get_barrier_semaphore(), me, z, col, planes, width, False)

    def copy_to(peer):
        return pltpu.make_async_remote_copy(
            src_ref=want.at[peer],
            dst_ref=got.at[col],
            send_sem=send.at[peer],
            recv_sem=recv.at[col],
            device_id=(z * width + peer,),
            device_id_type=MESH,
        )

    def arrival(peer):
        return pltpu.make_async_remote_copy(
            src_ref=want.at[peer],
            dst_ref=got.at[peer],
            send_sem=send.at[peer],
            recv_sem=recv.at[peer],
            device_id=(z * width + peer,),
            device_id_type=MESH,
        )

    @pl.loop(1, width)
    def _(step):
        copy_to(lax.rem(col + step, width)).start()

    got[col] = want[col]

    @pl.loop(1, width)
    def _(step):
        peer = lax.rem(col + step, width)
        arrival(peer).wait_recv()
        arrival(peer).wait_send()


def ask(want, planes):
    width = want.shape[0]
    return pl.pallas_call(
        functools.partial(ask_kernel, planes),
        out_shape=jax.ShapeDtypeStruct(want.shape, want.dtype),
        in_specs=[pl.BlockSpec(memory_space=pltpu.VMEM)],
        out_specs=pl.BlockSpec(memory_space=pltpu.VMEM),
        scratch_shapes=[pltpu.SemaphoreType.DMA((width,)), pltpu.SemaphoreType.DMA((width,))],
        compiler_params=pltpu.CompilerParams(collective_id=1, has_side_effects=True),
        name="ask",
    )(want)


def fetch_kernel(planes, slots, picks, source, out, mine, *scratch):
    below, above = scratch[: planes - 1], scratch[planes - 1 : 2 * planes - 2]
    pack, local, line_send, line_recv, send, recv, keep = scratch[2 * planes - 2 :]
    me, z, col, width = place(planes)
    greet(pltpu.get_barrier_semaphore(), me, z, col, planes, width, True)
    load = pltpu.make_async_copy(source, mine, local.at[0])
    load.start()

    def hop(way, dist):
        held = below if way == 0 else above
        return pltpu.make_async_remote_copy(
            src_ref=source if dist == 0 else held[dist - 1],
            dst_ref=held[dist],
            send_sem=line_send.at[way, dist],
            recv_sem=line_recv.at[way, dist],
            device_id=(me + width if way == 0 else me - width,),
            device_id_type=MESH,
        )

    def onward(way):
        return z < planes - 1 if way == 0 else z > 0

    def there(way, dist):
        return z - dist >= 0 if way == 0 else z + dist < planes

    def sent(peer, block, home):
        span = pl.ds(block * slots, slots)
        return pltpu.make_async_remote_copy(
            src_ref=pack.at[peer, span],
            dst_ref=out.at[home, span],
            send_sem=send.at[peer, block],
            recv_sem=recv.at[home, block],
            device_id=(z * width + peer,),
            device_id_type=MESH,
        )

    def kept(block):
        span = pl.ds(block * slots, slots)
        return pltpu.make_async_copy(pack.at[col, span], out.at[col, span], keep.at[block])

    def serve(held, block):
        @pl.loop(0, width)
        def _(step):
            peer = lax.rem(col + step, width)
            for slot in range(slots):
                at = block * slots + slot
                pack[peer, at] = held[picks[peer, at]]

        @pl.loop(1, width)
        def _(step):
            sent(lax.rem(col + step, width), block, col).start()

        kept(block).start()

    for way in range(2):
        if planes > 1:

            @pl.when(onward(way))
            def _():
                hop(way, 0).start()

    load.wait()
    serve(mine, z)
    for dist in range(1, planes):
        for way in range(2):

            @pl.when(there(way, dist))
            def _():
                hop(way, dist - 1).wait_recv()
                if dist < planes - 1:

                    @pl.when(onward(way))
                    def _():
                        hop(way, dist).start()

                serve((below if way == 0 else above)[dist - 1], z - dist if way == 0 else z + dist)

    for dist in range(planes - 1):
        for way in range(2):

            @pl.when(onward(way) & there(way, dist))
            def _():
                hop(way, dist).wait_send()

    @pl.loop(0, planes)
    def _(block):
        @pl.loop(1, width)
        def _(step):
            peer = lax.rem(col + step, width)
            sent(peer, block, peer).wait_recv()
            sent(peer, block, peer).wait_send()

        kept(block).wait()


def fetch(source, picks, planes, slots, ident):
    width = picks.shape[0]
    held = pltpu.VMEM(source.shape, source.dtype)
    slab = source.shape[1:]
    return pl.pallas_call(
        functools.partial(fetch_kernel, planes, slots),
        out_shape=jax.ShapeDtypeStruct((width, planes * slots) + slab, source.dtype),
        in_specs=[
            pl.BlockSpec(memory_space=pltpu.SMEM),
            pl.BlockSpec(memory_space=pl.ANY),
        ],
        out_specs=pl.BlockSpec(memory_space=pl.ANY),
        scratch_shapes=[held]
        + [held] * (2 * planes - 2)
        + [
            pltpu.VMEM((width, planes * slots) + slab, source.dtype),
            pltpu.SemaphoreType.DMA((1,)),
            pltpu.SemaphoreType.DMA((2, planes)),
            pltpu.SemaphoreType.DMA((2, planes)),
            pltpu.SemaphoreType.DMA((width, planes)),
            pltpu.SemaphoreType.DMA((width, planes)),
            pltpu.SemaphoreType.DMA((planes,)),
        ],
        compiler_params=pltpu.CompilerParams(
            collective_id=ident, has_side_effects=True, vmem_limit_bytes=VMEM_LIMIT
        ),
        name=f"fetch_{ident}",
    )(picks, source)


def farthest_first(planes, z, turn):
    block = 0
    for own in range(planes):
        order = sorted(range(planes), key=lambda b: (-abs(b - own), b))
        block = block + jnp.where(z == own, order[turn], 0)
    return block


def row_chunk(rows):
    return next(size for size in (64, 48, 32, 16, 8, rows) if rows % size == 0)


def reduce_kernel(planes, slots, table, outgoing, out, *scratch):
    landed = scratch[:planes]
    total, inbox, outbox, send, recv, keep, line_send, line_recv = scratch[planes:]
    me, z, col, width = place(planes)
    orbs, rows = total.shape[:2]
    chunk = row_chunk(rows)
    greet(pltpu.get_barrier_semaphore(), me, z, col, planes, width, True)

    def sent(peer, turn, home):
        span = pl.ds(farthest_first(planes, z, turn) * slots, slots)
        return pltpu.make_async_remote_copy(
            src_ref=outgoing.at[peer, span],
            dst_ref=landed[turn].at[pl.ds(home * slots, slots)],
            send_sem=send.at[peer, turn],
            recv_sem=recv.at[home, turn],
            device_id=(z * width + peer,),
            device_id_type=MESH,
        )

    def kept(turn):
        span = pl.ds(farthest_first(planes, z, turn) * slots, slots)
        return pltpu.make_async_copy(
            outgoing.at[col, span], landed[turn].at[pl.ds(col * slots, slots)], keep.at[turn]
        )

    def hop(way, block):
        return pltpu.make_async_remote_copy(
            src_ref=outbox.at[block],
            dst_ref=inbox.at[way, block],
            send_sem=line_send.at[block],
            recv_sem=line_recv.at[way, block],
            device_id=(me + width if way == 0 else me - width,),
            device_id_type=MESH,
        )

    for turn in range(planes):

        @pl.loop(1, width)
        def _(step):
            sent(lax.rem(col + step, width), turn, col).start()

        kept(turn).start()

    def add_line(way, block):
        hop(way, block).wait_recv()

        @pl.loop(0, orbs)
        def _(orb):
            for first in range(0, rows, chunk):
                part = pl.ds(first, chunk)
                total[orb, part] += inbox[way, block, orb, part].astype(jnp.float32)

    for turn in range(planes):
        block = farthest_first(planes, z, turn)

        @pl.loop(1, width)
        def _(step):
            peer = lax.rem(col + step, width)
            sent(peer, turn, peer).wait_recv()

        kept(turn).wait()

        @pl.loop(0, orbs)
        def _(orb):
            for first in range(0, rows, chunk):
                part = pl.ds(first, chunk)
                value = jnp.zeros((chunk, total.shape[2]), jnp.float32)
                for source in range(width):
                    at = table[block * orbs + orb, source]
                    slab = landed[turn][jnp.maximum(at, 0), part].astype(jnp.float32)
                    value = value + jnp.where(at >= 0, slab, 0.0)
                total[orb, part] = value

        if turn < planes - 1:
            for way in range(2):

                @pl.when(block > z if way == 0 else block < z)
                def _():
                    @pl.when(z > 0 if way == 0 else z < planes - 1)
                    def _():
                        add_line(way, block)

                    outbox[block] = total[...].astype(outbox.dtype)
                    hop(way, block).start()

        else:

            @pl.when(z > 0)
            def _():
                add_line(0, z)

            @pl.when(z < planes - 1)
            def _():
                add_line(1, z)

            out[...] = total[...].astype(out.dtype)

    for turn in range(planes):
        if turn < planes - 1:
            hop(0, farthest_first(planes, z, turn)).wait_send()

        @pl.loop(1, width)
        def _(step):
            sent(lax.rem(col + step, width), turn, col).wait_send()


def reduce_slots(outgoing, table, orbs, planes, slots):
    width = outgoing.shape[0]
    slab = outgoing.shape[2:]
    kind = outgoing.dtype
    return pl.pallas_call(
        functools.partial(reduce_kernel, planes, slots),
        out_shape=jax.ShapeDtypeStruct((orbs,) + slab, kind),
        in_specs=[
            pl.BlockSpec(memory_space=pltpu.SMEM),
            pl.BlockSpec(memory_space=pl.ANY),
        ],
        out_specs=pl.BlockSpec(memory_space=pltpu.VMEM),
        scratch_shapes=[pltpu.VMEM((width * slots,) + slab, kind)] * planes
        + [
            pltpu.VMEM((orbs,) + slab, jnp.float32),
            pltpu.VMEM((2, planes, orbs) + slab, kind),
            pltpu.VMEM((planes, orbs) + slab, kind),
            pltpu.SemaphoreType.DMA((width, planes)),
            pltpu.SemaphoreType.DMA((width, planes)),
            pltpu.SemaphoreType.DMA((planes,)),
            pltpu.SemaphoreType.DMA((planes,)),
            pltpu.SemaphoreType.DMA((2, planes)),
        ],
        compiler_params=pltpu.CompilerParams(
            collective_id=3, has_side_effects=True, vmem_limit_bytes=VMEM_LIMIT
        ),
        name="reduce_slots",
    )(table, outgoing)


def projections(factor_rows, masked):
    proj_i = jnp.einsum(
        "tavn,tabvr->tabrn", factor_rows[:, :4], masked, preferred_element_type=jnp.float32
    )
    proj_j = jnp.einsum(
        "tbvn,tabvr->tabrn", factor_rows[:, 4:], masked, preferred_element_type=jnp.float32
    )
    return (proj_i.astype(jnp.bfloat16), proj_j.astype(jnp.bfloat16))


def body(
    factors,
    orbital_owner,
    tile_orbitals,
    projectors,
    amplitudes,
    ranks,
    pair_energies,
    orbital_energies,
):
    dev_count = lax.axis_size("dev")
    planes = planes_of(dev_count)
    width = dev_count // planes
    tile_count = tile_orbitals.shape[0]
    orb_count, factor_width, aux_width = factors.shape
    rank_width = projectors.shape[2]
    need_count = tile_count * 7
    slots = -(-(8 * tile_count) // dev_count)
    my_orbitals = tile_orbitals.reshape(need_count)
    owner = orbital_owner[my_orbitals]
    entry = jnp.arange(need_count)
    same = (owner[:, None] == owner[None, :]) & (entry[None, :] < entry[:, None])
    slot = jnp.sum(same.astype(jnp.int32), axis=1)
    spot = lax.rem(owner, width) * (planes * slots) + lax.div(owner, width) * slots + slot
    hit = spot[None, :] == jnp.arange(dev_count * slots)[:, None]
    entry_at = jnp.sum(jnp.where(hit, entry[None, :], 0), axis=1)
    row_at = jnp.sum(jnp.where(hit, lax.div(my_orbitals, dev_count)[None, :] + 1, 0), axis=1) - 1
    want = jnp.zeros((width, 8, 128), jnp.int32)
    want = want.at[:, 0, : planes * slots].set(row_at.reshape(width, planes * slots))
    asked = ask(want, planes)[:, 0, : planes * slots]
    picks = jnp.maximum(asked, 0)
    by_plane = asked.reshape(width, planes, slots).transpose(1, 0, 2)
    match = by_plane[:, None] == jnp.arange(orb_count)[None, :, None, None]
    slot_code = jnp.arange(width * slots).reshape(width, slots)
    table = jnp.sum(jnp.where(match, slot_code + 1, 0), axis=3) - 1
    table = table.reshape(planes * orb_count, width)
    arrived = fetch(factors, picks, planes, slots, 2)
    arrived = arrived.reshape(dev_count * slots, factor_width, aux_width)
    fetched = arrived[spot].reshape(tile_count, 7, factor_width, aux_width)
    rank_keep = jnp.arange(rank_width)[None, :] < ranks[:, None]
    masked = (projectors * rank_keep.astype(jnp.bfloat16)[:, None, :]).reshape(
        tile_count, 4, 3, factor_width, rank_width
    )
    proj_i, proj_j = projections(fetched, masked)
    amp_half = amplitudes.astype(jnp.bfloat16).reshape(tile_count, 4, 3, rank_width, rank_width)
    cycle_i = jnp.einsum(
        "tabrc,tabcn->tabrn", amp_half, proj_j, preferred_element_type=jnp.float32
    ).astype(jnp.bfloat16)
    cycle_j = jnp.einsum(
        "tabrc,tabrn->tabcn", amp_half, proj_i, preferred_element_type=jnp.float32
    ).astype(jnp.bfloat16)
    sum_i = jnp.einsum("tabvr,tabrn->tavn", masked, cycle_i, preferred_element_type=jnp.float32)
    sum_j = jnp.einsum("tabvr,tabrn->tbvn", masked, cycle_j, preferred_element_type=jnp.float32)
    partial_value = (
        jnp.concatenate([sum_i, sum_j], axis=1)
        .astype(jnp.bfloat16)
        .reshape(need_count, factor_width, aux_width)
    )
    outgoing = partial_value[entry_at].reshape(width, planes * slots, factor_width, aux_width)
    orbital_sums = reduce_slots(outgoing, table, orb_count, planes, slots)
    returned = fetch(orbital_sums, picks, planes, slots, 4)
    returned = returned.reshape(dev_count * slots, factor_width, aux_width)
    collected = returned[spot].reshape(tile_count, 7, factor_width, aux_width)
    corr_i, corr_j = projections(collected, masked)
    residual = jnp.einsum("tabrn,tabcn->tabrc", proj_i, proj_j, preferred_element_type=jnp.float32)
    residual = residual + jnp.einsum(
        "tabrn,tabcn->tabrc", proj_i, corr_j, preferred_element_type=jnp.float32
    )
    residual = residual + jnp.einsum(
        "tabrn,tabcn->tabrc", corr_i, proj_j, preferred_element_type=jnp.float32
    )
    energy = pair_energies.reshape(tile_count, 4, 3, rank_width)
    occ_gaps = orbital_energies[my_orbitals].reshape(tile_count, 7)
    denominator = energy[:, :, :, :, None] + energy[:, :, :, None, :]
    denominator = (
        denominator + occ_gaps[:, :4, None, None, None] + occ_gaps[:, None, 4:, None, None]
    )
    keep_float = rank_keep.astype(jnp.float32).reshape(tile_count, 4, 3, rank_width)
    updated = (
        -(keep_float[:, :, :, :, None] * keep_float[:, :, :, None, :]) * residual / denominator
    )
    return (updated.reshape(tile_count * 12, rank_width, rank_width), orbital_sums)


def solution(mesh):
    in_specs = (
        P("dev", None, None),
        P(),
        P("dev", None),
        P("dev", None, None),
        P("dev", None, None),
        P("dev"),
        P("dev", None),
        P(),
    )
    out_specs = (P("dev", None, None), P("dev", None, None))
    return jax.shard_map(body, mesh=mesh, in_specs=in_specs, out_specs=out_specs, check_vma=False)
```

time: 606 us -> 337 us (0.56)
  waiting for transfers between devices: 405 us -> 0 us
  Pallas kernels: 0 us -> 237 us
  blocking collectives: 40.5 us -> 0 us
  other arithmetic: 34.9 us -> 12.2 us
  local copies, waits for them, and re-layouts: 40.5 us -> 23.7 us
  starting transfers between devices: 14.1 us -> 0 us
    all_to_all x3 -> x0, waiting for transfers between devices: 405 us -> none  [the longest x1 139 us: body(): lax.all_to_all(outgoing, 'dev', split_axis=0, concat_axis=0, tiled=True)]
    pallas_call x0 -> x4, Pallas kernels: none -> 237 us  [the longest x2 154 us: fetch(): pl.pallas_call(functools.partial(fetch_kernel, planes, slots), out_shape=...]
    unnamed x1 -> x0, blocking collectives: 40.5 us -> none
    select_n x8 -> x3, other arithmetic: 18 us -> 0.02 us  [the longest x1 0.01 us: body(): fetched = arrived[spot].reshape(tile_count, 7, factor_width, aux_width)]
    gather x7 -> x4, local copies, waits for them, and re-layouts: 36.9 us -> 19.4 us  [the longest x1 6.21 us: body(): partial_value[entry_at]]
    all_to_all x3 -> x0, starting transfers between devices: 14.1 us -> none  [the longest x1 5.71 us: body(): lax.all_to_all(pack_slots(factors, out_rows, out_valid), 'dev', split_axi...]
    dot_general x1 -> x0, matrix products: 6.2 us -> none  [body(): jnp.einsum('mq,qvn->mvn', selector, incoming.reshape(dev_count * slot_cap...]
  transfers between devices with their start and end apart: 3 -> 0, of which waited for: 3 -> 0; matrix products, arithmetic and copies ran while one was open for 2% -> 0% of each run, Pallas kernels for 0% -> 0%
where the time goes in v2:
time: 337 us; the launch traced here: 336 us
  Pallas kernels  237 us (70%)
  matrix products  62.2 us (18%)
  local copies, waits for them, and re-layouts  23.7 us (7%)
  other arithmetic  12.2 us (4%)
    pallas_call x2, Pallas kernels, fetch(): pl.pallas_call(functools.partial(fetch_kernel, planes, slots), out_shape=...  154 us
    pallas_call x1, Pallas kernels, reduce_slots(): pl.pallas_call(functools.partial(reduce_kernel, planes, slots), out_shape...  75.6 us
    dot_general x1, matrix products, body(): jnp.einsum('tabrn,tabcn->tabrc', proj_i, proj_j, preferred_element_type=j...  12.7 us
    dot_general x1, matrix products, body(): jnp.einsum('tabvr,tabrn->tbvn', masked, cycle_j, preferred_element_type=j...  8.9 us
    dot_general x1, matrix products, body(): jnp.einsum('tabrn,tabcn->tabrc', corr_i, proj_j, preferred_element_type=j...  8.72 us
    dot_general x1, matrix products, body(): jnp.einsum('tabrn,tabcn->tabrc', proj_i, corr_j, preferred_element_type=j...  8.48 us
    dot_general x1, matrix products, projections(): jnp.einsum('tbvn,tabvr->tabrn', factor_rows[:, 4:], masked, preferred_ele...  8.03 us
    dot_general x1, matrix products, projections(): jnp.einsum('tavn,tabvr->tabrn', factor_rows[:, :4], masked, preferred_ele...  7.87 us

profile of v2, /device:TPU:1, one launch (start us, length us, event | category | flops | bytes accessed | tf_op | source)
XLA Modules:
  0.0 336.2 jit_solution(6048310578132438231)
XLA Ops:
  0.6 0.0 copy-start
  0.6 0.8 reshape.286
  1.4 0.0 copy-done
  1.4 0.8 gather_fusion
  2.2 0.2 convert_reduce_fusion
  2.4 0.8 reshape.287
  3.2 0.1 select_reduce_fusion.1
  3.3 0.1 sub.13
  3.4 0.6 scatter.4.want
  4.0 7.3 %ask.1 = s32[8,8,128]{2,1,0:T(8,128)} custom-call(s32[8,8,128]{2,1,0:T(8,128)} %scatter.4.want), custom_call_target="tpu_custom_call" | custom-call | tf_op jit(solution)/shard_map/ask/pallas_call | solution.py:88
  11.3 1.4 fusion.62
  12.7 77.6 %fetch_2.1 = bf16[8,8,192,256]{3,2,1,0:T(8,128)(2,1)} custom-call(s32[8,8]{1,0:T(8,128)} %bitcast.107, bf16[8,192,256]{2,1,0:T(8,128)(2,1)} %source.1), custom_call_target="tpu_custom_call" | custom-call | tf_op jit(solution)/shard_map/fetch_2/pallas_call | solution.py:198
  90.3 0.0 copy-start.6
  90.3 6.2 %gather_fusion.1 = bf16[56,192,256]{2,1,0:T(8,128)(2,1)} fusion(bf16[64,192,256]{2,1,0:T(8,128)(2,1)} %bitcast.97, s32[1024]{0:T(1024)S(1)} %pad_clamp_fusion.1), kind=kCustom, calls=%fused_computation.1 | custom fusion | bytes 11010272 | tf_op jit(solution)/shard_map/gather | solution.py:420
  96.6 0.0 copy-done.6
  96.6 0.1 fusion.55
  96.6 0.0 slice-start
  96.7 2.8 broadcast_multiply_fusion
  99.5 0.0 copy-start.3
  99.5 0.0 slice-start.1
  99.5 8.0 %convert_bitcast_fusion = bf16[8,4,3,128,256]{4,3,1,2,0:T(8,128)(2,1)} fusion(bf16[8,4,3,192,128]{4,3,2,1,0:T(8,128)(2,1)S(1)} %bitcast.89, bf16[8,7,192,256]{3,2,1,0:T(8,128)(2,1)} %bitcast.99), kind=kOutput, calls=%fused_computation.20 | convolution fusion | flops 1211105280 | bytes 13369344 | tf_op jit(solution)/shard_map/tbvn,tabvr->tabrn/dot_general | solution.py:376
  107.5 0.0 copy-done.3
  107.5 0.0 slice-done
  107.5 0.0 slice-done.1
  107.5 2.3 convert_element_type.65
  109.9 7.4 %bitcast_convert_fusion = bf16[8,4,192,256]{3,2,1,0:T(8,128)(2,1)S(1)} fusion(bf16[8,4,3,192,128]{4,3,2,1,0:T(8,128)(2,1)} %bitcast.90, bf16[8,4,3,128,128]{4,3,2,1,0:T(8,128)(2,1)} %bitcast.105, bf16[8,4,3,128,256]{4,3,1,2,0:T(8,128)(2,1)} %convert_bitcast_fusion), kind=kOutput, calls=%fused_computation.11 | convolution fusion | flops 2017984512 | bytes 17301504 | tf_op jit(solution)/shard_map/tabvr,tabrn->tavn/dot_general | solution.py:433
  117.3 7.9 %convolution_convert_fusion = bf16[8,4,3,128,256]{4,3,2,1,0:T(8,128)(2,1)} fusion(bf16[8,4,3,192,128]{4,3,2,1,0:T(8,128)(2,1)} %bitcast.91, bf16[8,7,192,256]{3,2,1,0:T(8,128)(2,1)} %bitcast.100), kind=kOutput, calls=%fused_computation.33 | convolution fusion | flops 1211105280 | bytes 14155776 | tf_op jit(solution)/shard_map/tavn,tabvr->tabrn/dot_general | solution.py:373
  125.2 8.9 %bitcast_convert_fusion.1 = bf16[8,3,192,256]{3,2,1,0:T(8,128)(2,1)} fusion(bf16[8,4,3,128,128]{4,3,2,1,0:T(8,128)(2,1)} %bitcast.106, bf16[8,4,3,128,256]{4,3,2,1,0:T(8,128)(2,1)} %convolution_convert_fusion, bf16[8,4,3,192,128]{4,3,2,1,0:T(8,128)(2,1)} %bitcast.92), kind=kOutput, calls=%fused_computation.27 | convolution fusion | flops 2017591296 | bytes 16515072 | tf_op jit(solution)/shard_map/tabvr,tabrn->tbvn/dot_general | solution.py:434
  134.1 4.5 %pad_maximum_fusion = bf16[8,7,192,256]{3,2,1,0:T(8,128)(2,1)} fusion(bf16[8,3,192,256]{3,2,1,0:T(8,128)(2,1)} %bitcast_convert_fusion.1, bf16[8,4,192,256]{3,2,1,0:T(8,128)(2,1)S(1)} %bitcast_convert_fusion), kind=kLoop, calls=%fused_computation.21 | loop fusion | flops 2752512 | bytes 11010048 | tf_op jit(solution)/shard_map/concatenate | solution.py:436
  138.6 6.2 %gather_fusion.2 = bf16[64,192,256]{2,1,0:T(8,128)(2,1)} fusion(bf16[56,192,256]{2,1,0:T(8,128)(2,1)} %bitcast.95, s32[1024]{0:T(1024)S(1)} %pad_clamp_fusion), kind=kCustom, calls=%fused_computation.2 | custom fusion | bytes 12583168 | tf_op jit(solution)/shard_map/gather | solution.py:440
  144.8 0.1 copy.27
  144.9 0.6 add_bitcast_fusion.table
  145.5 75.6 %reduce_slots.1.source = bf16[8,192,256]{2,1,0:T(8,128)(2,1)} custom-call(s32[32,8]{1,0:T(8,128)} %add_bitcast_fusion.table, bf16[8,8,192,256]{3,2,1,0:T(8,128)(2,1)} %bitcast.96), custom_call_target="tpu_custom_call" | custom-call | tf_op jit(solution)/shard_map/reduce_slots/pallas_call | solution.py:346
  221.2 76.8 %fetch_4.1 = bf16[8,8,192,256]{3,2,1,0:T(8,128)(2,1)} custom-call(s32[8,8]{1,0:T(8,128)} %bitcast.108, bf16[8,192,256]{2,1,0:T(8,128)(2,1)} %reduce_slots.1.source), custom_call_target="tpu_custom_call" | custom-call | tf_op jit(solution)/shard_map/fetch_4/pallas_call | solution.py:198
  298.0 6.2 %gather_fusion.3 = bf16[56,192,256]{2,1,0:T(8,128)(2,1)} fusion(bf16[64,192,256]{2,1,0:T(8,128)(2,1)} %bitcast.98, s32[1024]{0:T(1024)S(1)} %pad_clamp_fusion.1), kind=kCustom, calls=%fused_computation.3 | custom fusion | bytes 11010272 | tf_op jit(solution)/shard_map/gather | solution.py:444
  304.1 8.5 %fusion = f32[8,4,3,128,128]{4,3,2,1,0:T(8,128)} fusion(bf16[8,4,3,128,256]{4,3,2,1,0:T(8,128)(2,1)} %convolution_convert_fusion, bf16[8,4,3,192,128]{4,3,2,1,0:T(8,128)(2,1)} %bitcast.93, bf16[8,7,192,256]{3,2,1,0:T(8,128)(2,1)} %bitcast.101), kind=kOutput, calls=%fused_computation.5 | convolution fusion | flops 2016411648 | bytes 19660800 | tf_op jit(solution)/shard_map/tabrn,tabcn->tabrc/dot_general | solution.py:447
  312.6 8.7 %fusion.8 = f32[8,4,3,128,128]{4,3,2,1,0:T(8,128)} fusion(bf16[8,4,3,128,256]{4,3,1,2,0:T(8,128)(2,1)} %convert_bitcast_fusion, bf16[8,4,3,192,128]{4,3,2,1,0:T(8,128)(2,1)} %bitcast.94, bf16[8,7,192,256]{3,2,1,0:T(8,128)(2,1)} %bitcast.102), kind=kOutput, calls=%fused_computation.15 | convolution fusion | flops 2016411648 | bytes 20447232 | tf_op jit(solution)/shard_map/tabrn,tabcn->tabrc/dot_general | solution.py:450
  321.3 0.0 copy-done.2
  321.3 0.8 gather_fusion.4
  322.1 0.1 reshape.297
  322.2 0.1 slice.50
  322.3 0.1 lt.82
  322.4 0.1 fusion.54
  322.5 0.0 copy-done.5
  322.6 0.0 copy-start.4
  322.6 0.0 copy-start.1
  322.6 12.7 %add_divide_fusion = f32[8,4,3,128,128]{4,3,2,1,0:T(8,128)} fusion(f32[8,4,3,128,128]{4,3,2,1,0:T(8,128)} %fusion.8, f32[8,4,3,128,128]{4,3,2,1,0:T(8,128)} %fusion, f32[8,3]{1,0:T(8,128)S(1)} %slice.50, f32[8,4]{1,0:T(8,128)S(1)} %bitcast.110, f32[8,4,3,128]{3,2,1,0:T(4,128)S(1)} %add.149, f32[8,4,3,128]{3,2,1,0:T(4,128)S(1)} %fusion.54, ...), kind=kOutput, calls=%fused_computation.14 | convolution fusion | flops 819462144 | bytes 31555808 | tf_op jit(solution)/shard_map/tabrn,tabcn->tabrc/dot_general | solution.py:446
  335.3 0.9 copy.86
  (16 shorter events, 0.1 us)
Async XLA Ops:
  0.6 0.8 copy-start
  90.3 6.3 %copy-start.6 = (s32[96]{0:T(128)S(1)}, s32[96]{0:T(128)}, u32[]{:S(2)}) copy-start(s32[96]{0:T(128)} %param.15) | copy-start | bytes 1156
  96.6 10.9 %slice-start = ((s8[6291456]{0:T(1024)(128)(4,1)}), s8[4194304]{0:T(1024)(128)(4,1)S(1)}, s32[]{:S(2)}) async-start(s8[6291456]{0:T(1024)(128)(4,1)} %bitcast.103), calls=%async_computation | async-start | bytes 8388608
  99.5 8.1 %copy-start.3 = (bf16[96,192,128]{2,1,0:T(8,128)(2,1)}, bf16[96,192,128]{2,1,0:T(8,128)(2,1)S(1)}, u32[]{:S(2)}) copy-start(bf16[96,192,128]{2,1,0:T(8,128)(2,1)S(1)} %broadcast_multiply_fusion) | copy-start | bytes 14155780
  99.5 8.1 %slice-start.1 = ((s8[6291456]{0:T(1024)(128)(4,1)}), s8[2097152]{0:T(1024)(128)(4,1)S(1)}, s32[]{:S(2)}) async-start(s8[6291456]{0:T(1024)(128)(4,1)} %bitcast.103), calls=%async_computation.1 | async-start | bytes 4194304
  312.6 8.7 %copy-start.2 = (f32[256]{0:T(256)S(1)}, f32[256]{0:T(256)}, u32[]{:S(2)}) copy-start(f32[256]{0:T(256)} %param.17) | copy-start | bytes 3076
  312.6 9.9 %copy-start.5 = (f32[96,128]{1,0:T(8,128)S(1)}, f32[96,128]{1,0:T(8,128)}, u32[]{:S(2)}) copy-start(f32[96,128]{1,0:T(8,128)} %param.16) | copy-start | bytes 147460
  322.6 12.8 %copy-start.4 = (bf16[8,192,256]{2,1,0:T(8,128)(2,1)S(1)}, bf16[8,192,256]{2,1,0:T(8,128)(2,1)}, u32[]{:S(2)}) copy-start(bf16[8,192,256]{2,1,0:T(8,128)(2,1)} %reduce_slots.1.source) | copy-start | bytes 2359300
  322.6 13.6 %copy-start.1 = (s32[256]{0:T(256)S(1)}, s32[256]{0:T(256)}, u32[]{:S(2)}) copy-start(s32[256]{0:T(256)} %param.11) | copy-start | bytes 3076

commit v3 on v2

--- a/solution.py
+++ b/solution.py
@@ -369,14 +369,178 @@
     )(table, outgoing)
 
 
-def projections(factor_rows, masked):
-    proj_i = jnp.einsum(
-        "tavn,tabvr->tabrn", factor_rows[:, :4], masked, preferred_element_type=jnp.float32
+LEFT, RIGHT = 4, 3
+PAIRS_TILE = LEFT * RIGHT
+
+
+def masked_blocks(ranks, projectors, tile):
+    kept = []
+    for pair in range(PAIRS_TILE):
+        value = projectors[pair]
+        lane = lax.broadcasted_iota(jnp.int32, value.shape, 1)
+        kept.append(jnp.where(lane < ranks[tile * PAIRS_TILE + pair], value, jnp.zeros_like(value)))
+    return kept
+
+
+def project(turned, slabs, left_out, right_out):
+    width = turned[0].shape[0]
+    for a in range(LEFT):
+        stack = jnp.concatenate([turned[RIGHT * a + b] for b in range(RIGHT)], axis=0)
+        value = jnp.dot(stack, slabs[a][0], preferred_element_type=jnp.float32)
+        value = value.astype(left_out.dtype)
+        for b in range(RIGHT):
+            left_out[RIGHT * a + b] = value[b * width : (b + 1) * width]
+    for b in range(RIGHT):
+        stack = jnp.concatenate([turned[RIGHT * a + b] for a in range(LEFT)], axis=0)
+        value = jnp.dot(stack, slabs[LEFT + b][0], preferred_element_type=jnp.float32)
+        value = value.astype(right_out.dtype)
+        for a in range(LEFT):
+            right_out[RIGHT * a + b] = value[a * width : (a + 1) * width]
+
+
+def cycle_kernel(spot, ranks, *refs):
+    slabs = refs[: LEFT + RIGHT]
+    projectors, amplitudes, out, left, right, staged, sems = refs[LEFT + RIGHT :]
+    tile = pl.program_id(0)
+    half = lax.rem(tile, 2)
+
+    def put(at, which, entry):
+        target = out.at[spot[at * (LEFT + RIGHT) + entry]]
+        return pltpu.make_async_copy(staged.at[which, entry], target, sems.at[which, entry])
+
+    kept = masked_blocks(ranks, projectors, tile)
+    project([value.T for value in kept], slabs, left, right)
+    for pair in range(PAIRS_TILE):
+        amp = amplitudes[pair].astype(jnp.bfloat16)
+        from_right = jnp.dot(amp, right[pair], preferred_element_type=jnp.float32)
+        from_left = jnp.dot(amp.T, left[pair], preferred_element_type=jnp.float32)
+        left[pair] = from_right.astype(left.dtype)
+        right[pair] = from_left.astype(right.dtype)
+
+    @pl.when(tile >= 2)
+    def _():
+        for entry in range(LEFT + RIGHT):
+            put(tile - 2, half, entry).wait()
+
+    for entry in range(LEFT + RIGHT):
+        if entry < LEFT:
+            pairs, cycles = [RIGHT * entry + b for b in range(RIGHT)], left
+        else:
+            pairs, cycles = [RIGHT * a + entry - LEFT for a in range(LEFT)], right
+        wide = jnp.concatenate([kept[pair] for pair in pairs], axis=1)
+        tall = jnp.concatenate([cycles[pair] for pair in pairs], axis=0)
+        value = jnp.dot(wide, tall, preferred_element_type=jnp.float32)
+        staged[half, entry] = value.astype(staged.dtype)
+        put(tile, half, entry).start()
+
+    @pl.when(tile == pl.num_programs(0) - 1)
+    def _():
+        for entry in range(LEFT + RIGHT):
+            put(tile, half, entry).wait()
+
+        @pl.when(tile >= 1)
+        def _():
+            for entry in range(LEFT + RIGHT):
+                put(tile - 1, 1 - half, entry).wait()
+
+
+def slab_specs(slab):
+    def at(entry):
+        return lambda tile, spot, *_: (spot[tile * (LEFT + RIGHT) + entry], 0, 0)
+
+    return [pl.BlockSpec((1,) + slab, at(entry)) for entry in range(LEFT + RIGHT)]
+
+
+def cycles(spot, ranks, arrived, projectors, amplitudes):
+    slab = arrived.shape[1:]
+    wide = projectors.shape[2]
+    held = pltpu.VMEM((PAIRS_TILE, wide, slab[1]), arrived.dtype)
+    grid_spec = pltpu.PrefetchScalarGridSpec(
+        num_scalar_prefetch=2,
+        grid=(projectors.shape[0] // PAIRS_TILE,),
+        in_specs=slab_specs(slab)
+        + [
+            pl.BlockSpec((PAIRS_TILE,) + projectors.shape[1:], lambda tile, *_: (tile, 0, 0)),
+            pl.BlockSpec((PAIRS_TILE,) + amplitudes.shape[1:], lambda tile, *_: (tile, 0, 0)),
+        ],
+        out_specs=pl.BlockSpec(memory_space=pl.ANY),
+        scratch_shapes=[
+            held,
+            held,
+            pltpu.VMEM((2, LEFT + RIGHT) + slab, arrived.dtype),
+            pltpu.SemaphoreType.DMA((2, LEFT + RIGHT)),
+        ],
     )
-    proj_j = jnp.einsum(
-        "tbvn,tabvr->tabrn", factor_rows[:, 4:], masked, preferred_element_type=jnp.float32
+    return pl.pallas_call(
+        cycle_kernel,
+        out_shape=jax.ShapeDtypeStruct(arrived.shape, arrived.dtype),
+        grid_spec=grid_spec,
+        compiler_params=pltpu.CompilerParams(vmem_limit_bytes=VMEM_LIMIT),
+        name="cycles",
+    )(spot, ranks, *[arrived] * (LEFT + RIGHT), projectors, amplitudes)
+
+
+def update_kernel(spot, ranks, orbitals, levels, *refs):
+    count = LEFT + RIGHT
+    slabs, sums = refs[:count], refs[count : 2 * count]
+    projectors, energies, out, left, right, left_sum, right_sum = refs[2 * count :]
+    tile = pl.program_id(0)
+    turned = [value.T for value in masked_blocks(ranks, projectors, tile)]
+    project(turned, slabs, left, right)
+    project(turned, sums, left_sum, right_sum)
+    across = (((1,), (1,)), ((), ()))
+
+    def product(a, b):
+        return lax.dot_general(a, b, across, preferred_element_type=jnp.float32)
+
+    for pair in range(PAIRS_TILE):
+        residual = product(left[pair], right[pair])
+        residual = residual + product(left[pair], right_sum[pair])
+        residual = residual + product(left_sum[pair], right[pair])
+        along = jnp.broadcast_to(energies[0, pair : pair + 1], residual.shape)
+        gap = along.T + along
+        gap = gap + levels[orbitals[tile * count + pair // RIGHT]]
+        gap = gap + levels[orbitals[tile * count + LEFT + pair % RIGHT]]
+        rank = ranks[tile * PAIRS_TILE + pair]
+        kept = lax.broadcasted_iota(jnp.int32, residual.shape, 0) < rank
+        kept = kept & (lax.broadcasted_iota(jnp.int32, residual.shape, 1) < rank)
+        out[pair] = jnp.where(kept, -residual / gap, 0.0)
+
+
+def update(spot, ranks, orbitals, levels, arrived, returned, projectors, pair_energies):
+    slab = arrived.shape[1:]
+    wide = projectors.shape[2]
+    tiles = projectors.shape[0] // PAIRS_TILE
+    held = pltpu.VMEM((PAIRS_TILE, wide, slab[1]), arrived.dtype)
+    grid_spec = pltpu.PrefetchScalarGridSpec(
+        num_scalar_prefetch=4,
+        grid=(tiles,),
+        in_specs=slab_specs(slab)
+        + slab_specs(slab)
+        + [
+            pl.BlockSpec((PAIRS_TILE,) + projectors.shape[1:], lambda tile, *_: (tile, 0, 0)),
+            pl.BlockSpec((1, PAIRS_TILE, wide), lambda tile, *_: (tile, 0, 0)),
+        ],
+        out_specs=pl.BlockSpec((PAIRS_TILE, wide, wide), lambda tile, *_: (tile, 0, 0)),
+        scratch_shapes=[held] * 4,
     )
-    return (proj_i.astype(jnp.bfloat16), proj_j.astype(jnp.bfloat16))
+    count = LEFT + RIGHT
+    return pl.pallas_call(
+        update_kernel,
+        out_shape=jax.ShapeDtypeStruct((tiles * PAIRS_TILE, wide, wide), jnp.float32),
+        grid_spec=grid_spec,
+        compiler_params=pltpu.CompilerParams(vmem_limit_bytes=VMEM_LIMIT),
+        name="update",
+    )(
+        spot,
+        ranks,
+        orbitals,
+        levels,
+        *[arrived] * count,
+        *[returned] * count,
+        projectors,
+        pair_energies.reshape(tiles, PAIRS_TILE, wide),
+    )
 
 
 def body(
@@ -394,7 +558,6 @@
     width = dev_count // planes
     tile_count = tile_orbitals.shape[0]
     orb_count, factor_width, aux_width = factors.shape
-    rank_width = projectors.shape[2]
     need_count = tile_count * 7
     slots = -(-(8 * tile_count) // dev_count)
     my_orbitals = tile_orbitals.reshape(need_count)
@@ -404,7 +567,6 @@
     slot = jnp.sum(same.astype(jnp.int32), axis=1)
     spot = lax.rem(owner, width) * (planes * slots) + lax.div(owner, width) * slots + slot
     hit = spot[None, :] == jnp.arange(dev_count * slots)[:, None]
-    entry_at = jnp.sum(jnp.where(hit, entry[None, :], 0), axis=1)
     row_at = jnp.sum(jnp.where(hit, lax.div(my_orbitals, dev_count)[None, :] + 1, 0), axis=1) - 1
     want = jnp.zeros((width, 8, 128), jnp.int32)
     want = want.at[:, 0, : planes * slots].set(row_at.reshape(width, planes * slots))
@@ -417,50 +579,15 @@
     table = table.reshape(planes * orb_count, width)
     arrived = fetch(factors, picks, planes, slots, 2)
     arrived = arrived.reshape(dev_count * slots, factor_width, aux_width)
-    fetched = arrived[spot].reshape(tile_count, 7, factor_width, aux_width)
-    rank_keep = jnp.arange(rank_width)[None, :] < ranks[:, None]
-    masked = (projectors * rank_keep.astype(jnp.bfloat16)[:, None, :]).reshape(
-        tile_count, 4, 3, factor_width, rank_width
-    )
-    proj_i, proj_j = projections(fetched, masked)
-    amp_half = amplitudes.astype(jnp.bfloat16).reshape(tile_count, 4, 3, rank_width, rank_width)
-    cycle_i = jnp.einsum(
-        "tabrc,tabcn->tabrn", amp_half, proj_j, preferred_element_type=jnp.float32
-    ).astype(jnp.bfloat16)
-    cycle_j = jnp.einsum(
-        "tabrc,tabrn->tabcn", amp_half, proj_i, preferred_element_type=jnp.float32
-    ).astype(jnp.bfloat16)
-    sum_i = jnp.einsum("tabvr,tabrn->tavn", masked, cycle_i, preferred_element_type=jnp.float32)
-    sum_j = jnp.einsum("tabvr,tabrn->tbvn", masked, cycle_j, preferred_element_type=jnp.float32)
-    partial_value = (
-        jnp.concatenate([sum_i, sum_j], axis=1)
-        .astype(jnp.bfloat16)
-        .reshape(need_count, factor_width, aux_width)
-    )
-    outgoing = partial_value[entry_at].reshape(width, planes * slots, factor_width, aux_width)
+    outgoing = cycles(spot, ranks, arrived, projectors, amplitudes)
+    outgoing = outgoing.reshape(width, planes * slots, factor_width, aux_width)
     orbital_sums = reduce_slots(outgoing, table, orb_count, planes, slots)
     returned = fetch(orbital_sums, picks, planes, slots, 4)
     returned = returned.reshape(dev_count * slots, factor_width, aux_width)
-    collected = returned[spot].reshape(tile_count, 7, factor_width, aux_width)
-    corr_i, corr_j = projections(collected, masked)
-    residual = jnp.einsum("tabrn,tabcn->tabrc", proj_i, proj_j, preferred_element_type=jnp.float32)
-    residual = residual + jnp.einsum(
-        "tabrn,tabcn->tabrc", proj_i, corr_j, preferred_element_type=jnp.float32
+    updated = update(
+        spot, ranks, my_orbitals, orbital_energies, arrived, returned, projectors, pair_energies
     )
-    residual = residual + jnp.einsum(
-        "tabrn,tabcn->tabrc", corr_i, proj_j, preferred_element_type=jnp.float32
-    )
-    energy = pair_energies.reshape(tile_count, 4, 3, rank_width)
-    occ_gaps = orbital_energies[my_orbitals].reshape(tile_count, 7)
-    denominator = energy[:, :, :, :, None] + energy[:, :, :, None, :]
-    denominator = (
-        denominator + occ_gaps[:, :4, None, None, None] + occ_gaps[:, None, 4:, None, None]
-    )
-    keep_float = rank_keep.astype(jnp.float32).reshape(tile_count, 4, 3, rank_width)
-    updated = (
-        -(keep_float[:, :, :, :, None] * keep_float[:, :, :, None, :]) * residual / denominator
-    )
-    return (updated.reshape(tile_count * 12, rank_width, rank_width), orbital_sums)
+    return (updated, orbital_sums)
 
 
 def solution(mesh):

time: 337 us -> 283 us (0.84)
  matrix products: 62.2 us -> 0 us
  Pallas kernels: 237 us -> 274 us
  local copies, waits for them, and re-layouts: 23.7 us -> 5.44 us
  other arithmetic: 12.2 us -> 2.27 us
    dot_general x7 -> x0, matrix products: 62.2 us -> none  [the longest x1 12.7 us: body(): jnp.einsum('tabrn,tabcn->tabrc', proj_i, proj_j, preferred_element_type=j...]
    pallas_call x0 -> x2, Pallas kernels: none -> 36.3 us  [the longest x1 19 us: update(): pl.pallas_call(update_kernel, out_shape=jax.ShapeDtypeStruct((tiles * PAI...]
    gather x4 -> x0, local copies, waits for them, and re-layouts: 19.4 us -> none  [the longest x1 6.21 us: body(): partial_value[entry_at]]
    concatenate x1 -> x0, other arithmetic: 4.5 us -> none  [body(): jnp.concatenate([sum_i, sum_j], axis=1).astype(jnp.bfloat16)]
where the time goes in v3:
time: 283 us; the launch traced here: 282 us
  Pallas kernels  274 us (97%)
  local copies, waits for them, and re-layouts  5.44 us (2%)
    pallas_call x2, Pallas kernels, fetch(): pl.pallas_call(functools.partial(fetch_kernel, planes, slots), out_shape=...  154 us
    pallas_call x1, Pallas kernels, reduce_slots(): pl.pallas_call(functools.partial(reduce_kernel, planes, slots), out_shape...  75.7 us
    pallas_call x1, Pallas kernels, update(): pl.pallas_call(update_kernel, out_shape=jax.ShapeDtypeStruct((tiles * PAI...  19 us
    pallas_call x1, Pallas kernels, cycles(): pl.pallas_call(cycle_kernel, out_shape=jax.ShapeDtypeStruct(arrived.shape...  17.3 us
    pallas_call x1, Pallas kernels, ask(): pl.pallas_call(functools.partial(ask_kernel, planes), out_shape=jax.Shape...  7.31 us

profile of v3, /device:TPU:1, one launch (start us, length us, event | category | flops | bytes accessed | tf_op | source)
XLA Modules:
  0.0 282.1 jit_solution(289506239134347572)
XLA Ops:
  0.6 0.0 copy-start
  0.6 0.8 reshape.152.orbitals
  1.4 0.0 copy-start.2
  1.4 0.8 reshape.151
  2.2 0.0 copy-done
  2.2 0.8 gather_fusion
  3.0 0.2 convert_reduce_fusion
  3.2 0.0 copy-start.3
  3.2 0.1 select_reduce_fusion.1
  3.3 0.1 sub.13
  3.4 0.6 scatter.4.want
  4.0 7.3 %ask.1 = s32[8,8,128]{2,1,0:T(8,128)} custom-call(s32[8,8,128]{2,1,0:T(8,128)} %scatter.4.want), custom_call_target="tpu_custom_call" | custom-call | tf_op jit(solution)/shard_map/ask/pallas_call | solution.py:88
  11.4 1.3 fusion.4
  12.7 0.1 copy.17
  12.8 0.6 add_bitcast_fusion.table
  13.4 1.4 reshape.159.refs_15_
  14.8 77.6 %fetch_2.1 = bf16[8,8,192,256]{3,2,1,0:T(8,128)(2,1)} custom-call(s32[8,8]{1,0:T(8,128)} %bitcast.34, bf16[8,192,256]{2,1,0:T(8,128)(2,1)} %source.1), custom_call_target="tpu_custom_call" | custom-call | tf_op jit(solution)/shard_map/fetch_2/pallas_call | solution.py:198
  92.4 0.0 copy-done.3
  92.4 17.3 %cycles.1 = bf16[64,192,256]{2,1,0:T(8,128)(2,1)} custom-call(s32[56]{0:T(128)} %copy-done.3, s32[96]{0:T(128)} %ranks.3, bf16[64,192,256]{2,1,0:T(8,128)(2,1)} %bitcast.12, bf16[64,192,256]{2,1,0:T(8,128)(2,1)} %bitcast.13, bf16[64,192,256]{2,1,0:T(8,128)(2,1)} %bitcast.14, bf16[64,192,256]{2,1,0:T(8,128)(2,1)} %bitcast.15, bf16[64,192,256]{2,1,0:T(8,128)(2,1)} %bitcast.16, ...), custom_call_target="tpu_custom_call" | custom-call | tf_op jit(solution)/shard_map/cycles/pallas_call | solution.py:474
  109.8 0.0 copy-done.2
  109.8 75.7 %reduce_slots.1.source = bf16[8,192,256]{2,1,0:T(8,128)(2,1)} custom-call(s32[32,8]{1,0:T(8,128)} %add_bitcast_fusion.table, bf16[8,8,192,256]{3,2,1,0:T(8,128)(2,1)} %bitcast.33), custom_call_target="tpu_custom_call" | custom-call | tf_op jit(solution)/shard_map/reduce_slots/pallas_call | solution.py:346
  185.5 76.8 %fetch_4.1 = bf16[8,8,192,256]{3,2,1,0:T(8,128)(2,1)} custom-call(s32[8,8]{1,0:T(8,128)} %bitcast.35, bf16[8,192,256]{2,1,0:T(8,128)(2,1)} %reduce_slots.1.source), custom_call_target="tpu_custom_call" | custom-call | tf_op jit(solution)/shard_map/fetch_4/pallas_call | solution.py:198
  262.3 0.0 copy-start.1
  262.3 19.0 %update.1 = f32[96,128,128]{2,1,0:T(8,128)} custom-call(s32[56]{0:T(128)} %copy-done.3, s32[96]{0:T(128)} %ranks.3, s32[56]{0:T(128)} %copy-done.2, f32[256]{0:T(256)} %levels.1, bf16[64,192,256]{2,1,0:T(8,128)(2,1)} %bitcast.19, bf16[64,192,256]{2,1,0:T(8,128)(2,1)} %bitcast.20, bf16[64,192,256]{2,1,0:T(8,128)(2,1)} %bitcast.21, ...), custom_call_target="tpu_custom_call" | custom-call | tf_op jit(solution)/shard_map/update/pallas_call | solution.py:528
  281.2 0.0 copy-done.1
  281.3 0.9 copy.19
  (6 shorter events, 0.1 us)
Async XLA Ops:
  0.6 1.6 copy-start
  1.4 108.4 %copy-start.2 = (s32[56]{0:T(128)}, s32[56]{0:T(128)S(1)}, u32[]{:S(2)}) copy-start(s32[56]{0:T(128)S(1)} %reshape.152.orbitals) | copy-start | bytes 676
  3.2 89.2 %copy-start.3 = (s32[56]{0:T(128)}, s32[56]{0:T(128)S(1)}, u32[]{:S(2)}) copy-start(s32[56]{0:T(128)S(1)} %get-tuple-element.17.spot) | copy-start | bytes 676
  262.3 19.0 %copy-start.1 = (bf16[8,192,256]{2,1,0:T(8,128)(2,1)S(1)}, bf16[8,192,256]{2,1,0:T(8,128)(2,1)}, u32[]{:S(2)}) copy-start(bf16[8,192,256]{2,1,0:T(8,128)(2,1)} %reduce_slots.1.source) | copy-start | bytes 2359300

commit v4 on v3

--- a/solution.py
+++ b/solution.py
@@ -46,63 +46,50 @@
     pl.semaphore_wait(barrier, count)
 
 
-def ask_kernel(planes, want, got, send, recv):
+def fetch_kernel(planes, slots, want, source, out, got, mine, picks, local, ask_send, ask_recv, *scratch):
     me, z, col, width = place(planes)
-    greet(pltpu.get_barrier_semaphore(), me, z, col, planes, width, False)
-
-    def copy_to(peer):
+    load = pltpu.make_async_copy(source, mine, local.at[0])
+    load.start()
+    greet(pltpu.get_barrier_semaphore(), me, z, col, planes, width, True)
+
+    def asking(peer, home):
         return pltpu.make_async_remote_copy(
             src_ref=want.at[peer],
-            dst_ref=got.at[col],
-            send_sem=send.at[peer],
-            recv_sem=recv.at[col],
+            dst_ref=got.at[home],
+            send_sem=ask_send.at[peer],
+            recv_sem=ask_recv.at[home],
             device_id=(z * width + peer,),
             device_id_type=MESH,
         )
 
-    def arrival(peer):
-        return pltpu.make_async_remote_copy(
-            src_ref=want.at[peer],
-            dst_ref=got.at[peer],
-            send_sem=send.at[peer],
-            recv_sem=recv.at[peer],
-            device_id=(z * width + peer,),
-            device_id_type=MESH,
-        )
-
     @pl.loop(1, width)
     def _(step):
-        copy_to(lax.rem(col + step, width)).start()
+        asking(lax.rem(col + step, width), col).start()
 
     got[col] = want[col]
 
-    @pl.loop(1, width)
-    def _(step):
-        peer = lax.rem(col + step, width)
-        arrival(peer).wait_recv()
-        arrival(peer).wait_send()
-
-
-def ask(want, planes):
-    width = want.shape[0]
-    return pl.pallas_call(
-        functools.partial(ask_kernel, planes),
-        out_shape=jax.ShapeDtypeStruct(want.shape, want.dtype),
-        in_specs=[pl.BlockSpec(memory_space=pltpu.VMEM)],
-        out_specs=pl.BlockSpec(memory_space=pltpu.VMEM),
-        scratch_shapes=[pltpu.SemaphoreType.DMA((width,)), pltpu.SemaphoreType.DMA((width,))],
-        compiler_params=pltpu.CompilerParams(collective_id=1, has_side_effects=True),
-        name="ask",
-    )(want)
-
-
-def fetch_kernel(planes, slots, picks, source, out, mine, *scratch):
+    def ready():
+        @pl.loop(1, width)
+        def _(step):
+            peer = lax.rem(col + step, width)
+            asking(peer, peer).wait_recv()
+            asking(peer, peer).wait_send()
+
+        table = pltpu.make_async_copy(got, picks, local.at[1])
+        table.start()
+        table.wait()
+        load.wait()
+
+    def pick(peer, at):
+        return jnp.maximum(picks[peer, 0, at], 0)
+
+    spread(planes, slots, pick, source, out, mine, ready, scratch, True)
+
+
+def spread(planes, slots, pick, source, out, mine, ready, scratch, early=False):
     below, above = scratch[: planes - 1], scratch[planes - 1 : 2 * planes - 2]
-    pack, local, line_send, line_recv, send, recv, keep = scratch[2 * planes - 2 :]
+    pack, line_send, line_recv, send, recv, keep = scratch[2 * planes - 2 :]
     me, z, col, width = place(planes)
-    greet(pltpu.get_barrier_semaphore(), me, z, col, planes, width, True)
-    load = pltpu.make_async_copy(source, mine, local.at[0])
-    load.start()
 
     def hop(way, dist):
         held = below if way == 0 else above
@@ -136,13 +123,16 @@
         span = pl.ds(block * slots, slots)
         return pltpu.make_async_copy(pack.at[col, span], out.at[col, span], keep.at[block])
 
-    def serve(held, block):
+    def serve(held, block, depart=None):
         @pl.loop(0, width)
         def _(step):
             peer = lax.rem(col + step, width)
             for slot in range(slots):
                 at = block * slots + slot
-                pack[peer, at] = held[picks[peer, at]]
+                pack[peer, at] = held[pick(peer, at)]
+
+        if depart is not None:
+            depart()
 
         @pl.loop(1, width)
         def _(step):
@@ -150,15 +140,18 @@
 
         kept(block).start()
 
-    for way in range(2):
-        if planes > 1:
-
-            @pl.when(onward(way))
-            def _():
-                hop(way, 0).start()
-
-    load.wait()
-    serve(mine, z)
+    def depart():
+        for way in range(2):
+            if planes > 1:
+
+                @pl.when(onward(way))
+                def _():
+                    hop(way, 0).start()
+
+    if early:
+        depart()
+    ready()
+    serve(mine, z, None if early else depart)
     for dist in range(1, planes):
         for way in range(2):
 
@@ -191,34 +184,47 @@
         kept(block).wait()
 
 
-def fetch(source, picks, planes, slots, ident):
-    width = picks.shape[0]
-    held = pltpu.VMEM(source.shape, source.dtype)
+def spread_scratch(shape, kind, planes, slots, width):
+    return [pltpu.VMEM(shape, kind)] * (2 * planes - 2) + [
+        pltpu.VMEM((width, planes * slots) + shape[1:], kind),
+        pltpu.SemaphoreType.DMA((2, planes)),
+        pltpu.SemaphoreType.DMA((2, planes)),
+        pltpu.SemaphoreType.DMA((width, planes)),
+        pltpu.SemaphoreType.DMA((width, planes)),
+        pltpu.SemaphoreType.DMA((planes,)),
+    ]
+
+
+def fetch(source, want, planes, slots):
+    width = want.shape[0]
     slab = source.shape[1:]
     return pl.pallas_call(
         functools.partial(fetch_kernel, planes, slots),
-        out_shape=jax.ShapeDtypeStruct((width, planes * slots) + slab, source.dtype),
+        out_shape=(
+            jax.ShapeDtypeStruct((width, planes * slots) + slab, source.dtype),
+            jax.ShapeDtypeStruct(want.shape, want.dtype),
+        ),
         in_specs=[
-            pl.BlockSpec(memory_space=pltpu.SMEM),
+            pl.BlockSpec(memory_space=pltpu.VMEM),
             pl.BlockSpec(memory_space=pl.ANY),
         ],
-        out_specs=pl.BlockSpec(memory_space=pl.ANY),
-        scratch_shapes=[held]
-        + [held] * (2 * planes - 2)
-        + [
-            pltpu.VMEM((width, planes * slots) + slab, source.dtype),
-            pltpu.SemaphoreType.DMA((1,)),
-            pltpu.SemaphoreType.DMA((2, planes)),
-            pltpu.SemaphoreType.DMA((2, planes)),
-            pltpu.SemaphoreType.DMA((width, planes)),
-            pltpu.SemaphoreType.DMA((width, planes)),
-            pltpu.SemaphoreType.DMA((planes,)),
-        ],
+        out_specs=(
+            pl.BlockSpec(memory_space=pl.ANY),
+            pl.BlockSpec(memory_space=pltpu.VMEM),
+        ),
+        scratch_shapes=[
+            pltpu.VMEM(source.shape, source.dtype),
+            pltpu.SMEM(want.shape, want.dtype),
+            pltpu.SemaphoreType.DMA((2,)),
+            pltpu.SemaphoreType.DMA((width,)),
+            pltpu.SemaphoreType.DMA((width,)),
+        ]
+        + spread_scratch(source.shape, source.dtype, planes, slots, width),
         compiler_params=pltpu.CompilerParams(
-            collective_id=ident, has_side_effects=True, vmem_limit_bytes=VMEM_LIMIT
+            collective_id=2, has_side_effects=True, vmem_limit_bytes=VMEM_LIMIT
         ),
-        name=f"fetch_{ident}",
-    )(picks, source)
+        name="fetch",
+    )(want, source)
 
 
 def farthest_first(planes, z, turn):
@@ -233,9 +239,9 @@
     return next(size for size in (64, 48, 32, 16, 8, rows) if rows % size == 0)
 
 
-def reduce_kernel(planes, slots, table, outgoing, out, *scratch):
+def reduce_kernel(planes, slots, table, picks, outgoing, out, returned, *scratch):
     landed = scratch[:planes]
-    total, inbox, outbox, send, recv, keep, line_send, line_recv = scratch[planes:]
+    total, inbox, outbox, send, recv, keep, line_send, line_recv = scratch[planes : planes + 8]
     me, z, col, width = place(planes)
     orbs, rows = total.shape[:2]
     chunk = row_chunk(rows)
@@ -338,19 +344,31 @@
         def _(step):
             sent(lax.rem(col + step, width), turn, col).wait_send()
 
-
-def reduce_slots(outgoing, table, orbs, planes, slots):
+    def pick(peer, at):
+        return picks[peer, at]
+
+    spread(planes, slots, pick, out, returned, out, lambda: None, scratch[planes + 8 :])
+
+
+def reduce_slots(outgoing, table, picks, orbs, planes, slots):
     width = outgoing.shape[0]
     slab = outgoing.shape[2:]
     kind = outgoing.dtype
     return pl.pallas_call(
         functools.partial(reduce_kernel, planes, slots),
-        out_shape=jax.ShapeDtypeStruct((orbs,) + slab, kind),
+        out_shape=(
+            jax.ShapeDtypeStruct((orbs,) + slab, kind),
+            jax.ShapeDtypeStruct(outgoing.shape, kind),
+        ),
         in_specs=[
+            pl.BlockSpec(memory_space=pltpu.SMEM),
             pl.BlockSpec(memory_space=pltpu.SMEM),
             pl.BlockSpec(memory_space=pl.ANY),
         ],
-        out_specs=pl.BlockSpec(memory_space=pltpu.VMEM),
+        out_specs=(
+            pl.BlockSpec(memory_space=pltpu.VMEM),
+            pl.BlockSpec(memory_space=pl.ANY),
+        ),
         scratch_shapes=[pltpu.VMEM((width * slots,) + slab, kind)] * planes
         + [
             pltpu.VMEM((orbs,) + slab, jnp.float32),
@@ -361,12 +379,13 @@
             pltpu.SemaphoreType.DMA((planes,)),
             pltpu.SemaphoreType.DMA((planes,)),
             pltpu.SemaphoreType.DMA((2, planes)),
-        ],
+        ]
+        + spread_scratch((orbs,) + slab, kind, planes, slots, width),
         compiler_params=pltpu.CompilerParams(
             collective_id=3, has_side_effects=True, vmem_limit_bytes=VMEM_LIMIT
         ),
         name="reduce_slots",
-    )(table, outgoing)
+    )(table, picks, outgoing)
 
 
 LEFT, RIGHT = 4, 3
@@ -497,7 +516,8 @@
         residual = product(left[pair], right[pair])
         residual = residual + product(left[pair], right_sum[pair])
         residual = residual + product(left_sum[pair], right[pair])
-        along = jnp.broadcast_to(energies[0, pair : pair + 1], residual.shape)
+        own = energies[pl.ds(tile * PAIRS_TILE + pair, 1)]
+        along = jnp.broadcast_to(own, residual.shape)
         gap = along.T + along
         gap = gap + levels[orbitals[tile * count + pair // RIGHT]]
         gap = gap + levels[orbitals[tile * count + LEFT + pair % RIGHT]]
@@ -519,7 +539,7 @@
         + slab_specs(slab)
         + [
             pl.BlockSpec((PAIRS_TILE,) + projectors.shape[1:], lambda tile, *_: (tile, 0, 0)),
-            pl.BlockSpec((1, PAIRS_TILE, wide), lambda tile, *_: (tile, 0, 0)),
+            pl.BlockSpec(pair_energies.shape, lambda tile, *_: (0, 0)),
         ],
         out_specs=pl.BlockSpec((PAIRS_TILE, wide, wide), lambda tile, *_: (tile, 0, 0)),
         scratch_shapes=[held] * 4,
@@ -539,7 +559,7 @@
         *[arrived] * count,
         *[returned] * count,
         projectors,
-        pair_energies.reshape(tiles, PAIRS_TILE, wide),
+        pair_energies,
     )
 
 
@@ -570,19 +590,18 @@
     row_at = jnp.sum(jnp.where(hit, lax.div(my_orbitals, dev_count)[None, :] + 1, 0), axis=1) - 1
     want = jnp.zeros((width, 8, 128), jnp.int32)
     want = want.at[:, 0, : planes * slots].set(row_at.reshape(width, planes * slots))
-    asked = ask(want, planes)[:, 0, : planes * slots]
+    arrived, asked = fetch(factors, want, planes, slots)
+    asked = asked[:, 0, : planes * slots]
     picks = jnp.maximum(asked, 0)
     by_plane = asked.reshape(width, planes, slots).transpose(1, 0, 2)
     match = by_plane[:, None] == jnp.arange(orb_count)[None, :, None, None]
     slot_code = jnp.arange(width * slots).reshape(width, slots)
     table = jnp.sum(jnp.where(match, slot_code + 1, 0), axis=3) - 1
     table = table.reshape(planes * orb_count, width)
-    arrived = fetch(factors, picks, planes, slots, 2)
     arrived = arrived.reshape(dev_count * slots, factor_width, aux_width)
     outgoing = cycles(spot, ranks, arrived, projectors, amplitudes)
     outgoing = outgoing.reshape(width, planes * slots, factor_width, aux_width)
-    orbital_sums = reduce_slots(outgoing, table, orb_count, planes, slots)
-    returned = fetch(orbital_sums, picks, planes, slots, 4)
+    orbital_sums, returned = reduce_slots(outgoing, table, picks, orb_count, planes, slots)
     returned = returned.reshape(dev_count * slots, factor_width, aux_width)
     updated = update(
         spot, ranks, my_orbitals, orbital_energies, arrived, returned, projectors, pair_energies

time: 283 us -> 274 us (0.968)
  Pallas kernels: 274 us -> 266 us
    pallas_call x2 -> x1, Pallas kernels: 154 us -> 79.8 us  [fetch(): pl.pallas_call(functools.partial(fetch_kernel, planes, slots), out_shape=...]
    pallas_call x1, Pallas kernels: 75.7 us -> 150 us  [reduce_slots(): pl.pallas_call(functools.partial(reduce_kernel, planes, slots), out_shape...]
    pallas_call x1 -> x0, Pallas kernels: 7.31 us -> none  [ask(): pl.pallas_call(functools.partial(ask_kernel, planes), out_shape=jax.Shape...]
where the time goes in v4:
time: 274 us; the launch traced here: 273 us
  Pallas kernels  266 us (97%)
  local copies, waits for them, and re-layouts  4.01 us (1%)
    pallas_call x1, Pallas kernels, reduce_slots(): pl.pallas_call(functools.partial(reduce_kernel, planes, slots), out_shape...  150 us
    pallas_call x1, Pallas kernels, fetch(): pl.pallas_call(functools.partial(fetch_kernel, planes, slots), out_shape=...  79.8 us
    pallas_call x1, Pallas kernels, update(): pl.pallas_call(update_kernel, out_shape=jax.ShapeDtypeStruct((tiles * PAI...  18.9 us
    pallas_call x1, Pallas kernels, cycles(): pl.pallas_call(cycle_kernel, out_shape=jax.ShapeDtypeStruct(arrived.shape...  17.3 us

profile of v4, /device:TPU:1, one launch (start us, length us, event | category | flops | bytes accessed | tf_op | source)
XLA Modules:
  0.0 273.1 jit_solution(17537842518673131956)
XLA Ops:
  0.6 0.0 copy-start
  0.6 0.8 reshape.149.orbitals
  1.4 0.0 copy-start.2
  1.4 0.8 reshape.148
  2.2 0.0 copy-done
  2.2 0.8 gather_fusion
  3.0 0.2 convert_reduce_fusion
  3.2 0.0 copy-start.3
  3.2 0.1 select_reduce_fusion.1
  3.3 0.1 sub.13
  3.4 0.6 scatter.4.want
  4.0 79.8 %fetch.1 = (bf16[8,8,192,256]{3,2,1,0:T(8,128)(2,1)}, s32[8,8,128]{2,1,0:T(8,128)}) custom-call(s32[8,8,128]{2,1,0:T(8,128)} %scatter.4.want, bf16[8,192,256]{2,1,0:T(8,128)(2,1)} %source.1), custom_call_target="tpu_custom_call" | custom-call | tf_op jit(solution)/shard_map/fetch/pallas_call | solution.py:201
  83.8 1.3 broadcast_maximum_fusion
  85.2 0.1 copy.17
  85.2 0.6 add_bitcast_fusion.table
  85.8 0.0 copy-done.3
  85.8 17.3 %cycles.1 = bf16[64,192,256]{2,1,0:T(8,128)(2,1)} custom-call(s32[56]{0:T(128)} %copy-done.3, s32[96]{0:T(128)} %ranks.3, bf16[64,192,256]{2,1,0:T(8,128)(2,1)} %bitcast.12, bf16[64,192,256]{2,1,0:T(8,128)(2,1)} %bitcast.13, bf16[64,192,256]{2,1,0:T(8,128)(2,1)} %bitcast.14, bf16[64,192,256]{2,1,0:T(8,128)(2,1)} %bitcast.15, bf16[64,192,256]{2,1,0:T(8,128)(2,1)} %bitcast.16, ...), custom_call_target="tpu_custom_call" | custom-call | tf_op jit(solution)/shard_map/cycles/pallas_call | solution.py:493
  103.2 0.0 copy-done.2
  103.2 150.1 %reduce_slots.1 = (bf16[8,192,256]{2,1,0:T(8,128)(2,1)}, bf16[8,8,192,256]{3,2,1,0:T(8,128)(2,1)}) custom-call(s32[32,8]{1,0:T(8,128)} %add_bitcast_fusion.table, s32[8,8]{1,0:T(8,128)} %bitcast.36, bf16[8,8,192,256]{3,2,1,0:T(8,128)(2,1)} %bitcast.33), custom_call_target="tpu_custom_call" | custom-call | tf_op jit(solution)/shard_map/reduce_slots/pallas_call | solution.py:357
  253.3 0.0 copy-start.1
  253.3 18.9 %update.1 = f32[96,128,128]{2,1,0:T(8,128)} custom-call(s32[56]{0:T(128)} %copy-done.3, s32[96]{0:T(128)} %ranks.3, s32[56]{0:T(128)} %copy-done.2, f32[256]{0:T(256)} %levels.1, bf16[64,192,256]{2,1,0:T(8,128)(2,1)} %bitcast.19, bf16[64,192,256]{2,1,0:T(8,128)(2,1)} %bitcast.20, bf16[64,192,256]{2,1,0:T(8,128)(2,1)} %bitcast.21, ...), custom_call_target="tpu_custom_call" | custom-call | tf_op jit(solution)/shard_map/update/pallas_call | solution.py:548
  272.2 0.0 copy-done.1
  272.3 0.9 copy.19
  (6 shorter events, 0.1 us)
Async XLA Ops:
  0.6 1.6 copy-start
  1.4 101.8 %copy-start.2 = (s32[56]{0:T(128)}, s32[56]{0:T(128)S(1)}, u32[]{:S(2)}) copy-start(s32[56]{0:T(128)S(1)} %reshape.149.orbitals) | copy-start | bytes 676
  3.2 82.6 %copy-start.3 = (s32[56]{0:T(128)}, s32[56]{0:T(128)S(1)}, u32[]{:S(2)}) copy-start(s32[56]{0:T(128)S(1)} %get-tuple-element.25.spot) | copy-start | bytes 676
  253.3 19.0 %copy-start.1 = (bf16[8,192,256]{2,1,0:T(8,128)(2,1)S(1)}, bf16[8,192,256]{2,1,0:T(8,128)(2,1)}, u32[]{:S(2)}) copy-start(bf16[8,192,256]{2,1,0:T(8,128)(2,1)} %get-tuple-element.29) | copy-start | bytes 2359300
